TPU v7x, 32 devices: a whole 2x2x4 slice. The times are simulated.
32 devices in a mesh: grp: 1, row: 8 (over z, y), col: 4 (over x, core).
Axes of the slice: x: 2, y: 2, z: 4, core: 2. Of those that a mesh axis runs over, the one named last changes fastest.
Arguments:
- pair_act: bfloat16 [128, 128, 128], P(('grp', 'row'), 'col'), may hold values from -6 to 6
- single: bfloat16 [128, 768], P(('grp', 'row')), may hold values from -6 to 6
- token_mask: int32 [128], P('grp'), may hold values from 0 to 1, as said below
- chain_index: int32 [128], P('grp'), may hold values from 0 to 7, never falling along the last dimension, each value on 1 to 32 neighbouring positions
- residue_index: int32 [128], P('grp'), may hold values from 1 to 192, as said below
- tri_gain: float32 [2, 128], replicated, may hold values from 0.25 to 1.75
- tri_qk: bfloat16 [2, 128, 256], replicated, may hold values from -1.5 to 1.5
- tri_vg: bfloat16 [2, 128, 256], replicated, may hold values from -0.5 to 0.5
- tri_out: bfloat16 [2, 128, 128], replicated, may hold values from -0.5 to 0.5
- bias_gain: float32 [128], replicated, may hold values from 0.25 to 1.75
- bias_proj: bfloat16 [128, 16], replicated, may hold values from -0.5 to 0.5
- chain_bias: float32 [16], P('col'), may hold values from -4 to 4
- pos_slope: float32 [16], P('col'), may hold values from -6 to 6
- attn_gain: float32 [768], replicated, may hold values from 0.25 to 1.75
- attn_qk: bfloat16 [2, 768, 768], P(None, None, 'col'), may hold values from -0.375 to 0.375
- attn_vg: bfloat16 [2, 768, 768], P(None, None, 'col'), may hold values from -0.21875 to 0.21875
- attn_out: bfloat16 [768, 768], P('col'), may hold values from -0.875 to 0.875
Outputs:
- pair_out: bfloat16 [128, 128, 128], P(('grp', 'row'), 'col')
- token_update: bfloat16 [128, 768], P(('grp', 'row'), 'col')
Inputs may be any that keep to these rules, and one draw needn't show every extreme that they name: `token_mask`: 1 on a leading run of at least 64 positions, 0 on the rest, and some position is 0. `chain_index`: never decreasing along the positions; all 8 chains occur. `residue_index`: starts at 1 and rises by 1 or 2 from each position to the next, by 2 at exactly 64 of them.
All inputs are finite; a program needn't handle non-finite values.
Results may differ from a plain program's by a relative error of at most 0.019.
Values may be sent and summed in bfloat16 or wider, within the bound.
No kernel may reach another device: no remote copies, remote signals or barrier semaphores. Data moves between devices by JAX's collectives and lax.ppermute only.
A program may use at most 64 MiB of HBM per device.

v0:
```python
import math

import jax
import jax.numpy as jnp
from jax import lax
from jax.sharding import PartitionSpec as P

C = 128
TRI_HEADS = 8
TRI_DIM = 16
HEAD_DIM = 48


epsilon = 1e-05
cap_value = 10.0
rel_reach = 32.0
highest = lax.Precision.HIGHEST


def layer_norm(inputs, norm_gain):
    inputs = inputs.astype(jnp.float32)
    centered = inputs - jnp.mean(inputs, -1, keepdims=True)
    spread = jnp.mean(centered * centered, -1, keepdims=True)
    return centered * lax.rsqrt(spread + epsilon) * norm_gain


def feature(inputs):
    return jnp.where(inputs > 0, inputs + 1.0, jnp.exp(jnp.minimum(inputs, 0.0)))


def split_heads(inputs):
    return inputs.reshape(inputs.shape[:-1] + (TRI_HEADS, TRI_DIM))


def project(pair_tile, norm_gain, qk_weight, vg_weight):
    normed = layer_norm(pair_tile, norm_gain).astype(jnp.bfloat16)
    query_key = jnp.dot(normed, qk_weight, preferred_element_type=jnp.float32)
    value_gate = jnp.dot(normed, vg_weight, preferred_element_type=jnp.float32)
    return (
        feature(split_heads(query_key[..., :C])),
        feature(split_heads(query_key[..., C:])),
        split_heads(value_gate[..., :C]),
        value_gate[..., C:],
    )


def finish(pair_tile, mixed_heads, gate_part, out_weight):
    update = (jax.nn.sigmoid(gate_part) * mixed_heads.reshape(gate_part.shape)).astype(jnp.bfloat16)
    return (
        pair_tile.astype(jnp.float32)
        + jnp.dot(update, out_weight, preferred_element_type=jnp.float32)
    ).astype(jnp.bfloat16)


def on_device(
    pair_act,
    single,
    token_mask,
    chain_index,
    residue_index,
    tri_gain,
    tri_qk,
    tri_vg,
    tri_out,
    bias_gain,
    bias_proj,
    chain_bias,
    pos_slope,
    attn_gain,
    attn_qk,
    attn_vg,
    attn_out,
):
    tokens = token_mask.shape[0]
    row_count = pair_act.shape[0]
    col_count = pair_act.shape[1]
    row_first = lax.axis_index("row") * row_count
    col_first = lax.axis_index("col") * col_count
    mask_float = token_mask.astype(jnp.float32)
    row_mask = lax.dynamic_slice_in_dim(mask_float, row_first, row_count)
    col_mask = lax.dynamic_slice_in_dim(mask_float, col_first, col_count)
    tri_scale = 1.0 / (2.0 * TRI_DIM * math.sqrt(tokens))
    query_feat, key_feat, values, gate_part = project(pair_act, tri_gain[0], tri_qk[0], tri_vg[0])
    key_feat = key_feat * col_mask[None, :, None, None]
    states = jnp.einsum("ijhe,ijhf->ihef", key_feat, values, precision=highest)
    states = lax.psum(states.reshape(row_count, -1).astype(jnp.bfloat16), "col").astype(jnp.float32)
    states = states.reshape(row_count, TRI_HEADS, TRI_DIM, TRI_DIM)
    mixed_heads = tri_scale * jnp.einsum("ijhe,ihef->ijhf", query_feat, states, precision=highest)
    pair_first = finish(pair_act, mixed_heads, gate_part, tri_out[0])
    query_feat, key_feat, values, gate_part = project(pair_first, tri_gain[1], tri_qk[1], tri_vg[1])
    key_feat = key_feat * row_mask[:, None, None, None]
    col_sums = jnp.einsum("ijhe,ijhf->jhef", key_feat, values, precision=highest)
    col_sums = lax.psum(col_sums.reshape(col_count, -1).astype(jnp.bfloat16), "row").astype(
        jnp.float32
    )
    col_sums = col_sums.reshape(col_count, TRI_HEADS, TRI_DIM, TRI_DIM)
    mixed_heads = tri_scale * jnp.einsum("ijhe,jhef->ijhf", query_feat, col_sums, precision=highest)
    pair_second = finish(pair_first, mixed_heads, gate_part, tri_out[1])
    normed = layer_norm(pair_second, bias_gain).astype(jnp.bfloat16)
    tile_bias = jnp.einsum(
        "ijc,ch->hij", normed, bias_proj, preferred_element_type=jnp.float32
    ).astype(jnp.bfloat16)
    heads_here = chain_bias.shape[0]
    own_bias = lax.all_to_all(tile_bias, "col", split_axis=0, concat_axis=2, tiled=True)
    tok_normed = layer_norm(single, attn_gain).astype(jnp.bfloat16)
    query_rows = jnp.dot(tok_normed, attn_qk[0], preferred_element_type=jnp.float32).astype(
        jnp.bfloat16
    )
    key_rows = jnp.dot(tok_normed, attn_qk[1], preferred_element_type=jnp.float32).astype(
        jnp.bfloat16
    )
    value_rows = jnp.dot(tok_normed, attn_vg[0], preferred_element_type=jnp.float32).astype(
        jnp.bfloat16
    )
    gate_rows = jnp.dot(tok_normed, attn_vg[1], preferred_element_type=jnp.float32)
    local_width = query_rows.shape[1]
    query_heads = query_rows.reshape(row_count, heads_here, HEAD_DIM)
    my_chain = lax.dynamic_slice_in_dim(chain_index, row_first, row_count)
    my_residue = lax.dynamic_slice_in_dim(residue_index, row_first, row_count)
    piece_keys = lax.all_gather(key_rows, "row", axis=0, tiled=True)
    piece_values = lax.all_gather(value_rows, "row", axis=0, tiled=True)
    piece_rows = piece_keys.shape[0]
    key_heads = piece_keys.reshape(piece_rows, heads_here, HEAD_DIM)
    value_heads = piece_values.reshape(piece_rows, heads_here, HEAD_DIM)
    scores = jnp.einsum(
        "ihd,jhd->hij", query_heads, key_heads, preferred_element_type=jnp.float32
    ) / math.sqrt(HEAD_DIM)
    scores = scores + own_bias.astype(jnp.float32)
    same_chain = my_chain[:, None] == chain_index[None, :]
    offset = (
        jnp.clip(
            (my_residue[:, None] - residue_index[None, :]).astype(jnp.float32),
            -rel_reach,
            rel_reach,
        )
        / rel_reach
    )
    scores = scores + jnp.where(
        same_chain[None], chain_bias[:, None, None] + pos_slope[:, None, None] * offset[None], 0.0
    )
    weights = jnp.exp(cap_value * jnp.tanh(scores / cap_value)) * mask_float[None, None, :]
    numerator = jnp.einsum(
        "hij,jhd->ihd",
        weights.astype(jnp.bfloat16),
        value_heads,
        preferred_element_type=jnp.float32,
    )
    denominator = jnp.sum(weights, axis=2)
    numerator, denominator = (numerator, denominator)
    attended = numerator / jnp.transpose(denominator)[:, :, None]
    gated = (jax.nn.sigmoid(gate_rows) * attended.reshape(row_count, local_width)).astype(
        jnp.bfloat16
    )
    head_terms = jnp.dot(gated, attn_out, preferred_element_type=jnp.float32)
    token_update = lax.psum_scatter(
        head_terms.astype(jnp.bfloat16), "col", scatter_dimension=1, tiled=True
    )
    return (pair_second, token_update)


def solution(mesh):
    return jax.shard_map(
        on_device,
        mesh=mesh,
        in_specs=(
            P(("grp", "row"), "col", None),
            P(("grp", "row"), None),
            P("grp"),
            P("grp"),
            P("grp"),
            P(),
            P(),
            P(),
            P(),
            P(),
            P(),
            P("col"),
            P("col"),
            P(),
            P(None, None, "col"),
            P(None, None, "col"),
            P("col", None),
        ),
        out_specs=(P(("grp", "row"), "col", None), P(("grp", "row"), "col")),
        check_vma=False,
    )
```

profile of v0, /device:TPU:0, one launch (start us, length us, event | category | flops | bytes accessed | tf_op | source)
XLA Modules:
  0.0 226.2 jit_solution(9882278493999006250)
XLA Ops:
  7.3 0.7 convert_element_type.100
  8.0 1.0 convert_reduce_fusion
  9.1 1.2 fusion.33
  10.2 0.8 slice_bitcast_fusion
  11.0 1.2 fusion.57
  12.2 0.8 exponential_select_fusion.2
  13.1 0.3 copy.42
  13.4 0.3 fusion.59
  13.8 0.3 copy.43
  14.2 2.6 %convolution_convert_fusion.1 = bf16[16,8,16,16]{3,2,1,0:T(8,128)(2,1)} fusion(f32[16,32,8,16]{1,3,2,0:T(8,128)S(1)} %bitcast.93, f32[16,32,8,16]{1,3,2,0:T(8,128)S(1)} %bitcast.91, f32[32]{0:T(128)S(1)} %dynamic_slice.12), kind=kOutput, calls=%fused_computation.3 | convolution fusion | flops 12681216 | bytes 589952 | tf_op jit(solution)/shard_map/ijhe,ijhf->ihef/dot_general | solution.py:85
  17.1 0.2 fusion.73
  17.3 1.1 convolution_convert_fusion.4
  18.4 1.2 convolution_convert_fusion.5
  19.6 1.2 convolution_convert_fusion.6
  21.1 0.6 dynamic_slice.13
  21.7 0.3 copy.44
  22.0 32.7 %all_gather.7 = bf16[128,192]{1,0:T(8,128)(2,1)S(1)} all-gather(bf16[16,192]{1,0:T(8,128)(2,1)S(1)} %convolution_convert_fusion.4), channel_id=1, replica_groups=mesh['grp'=1,'row'=8,'col'=4] {'row'}, dimensions={0}, use_global_device_ids=true | all-gather | bytes 55296 | tf_op jit(solution)/shard_map/all_gather | solution.py:120
  54.9 0.6 dynamic_slice.14
  55.5 1.8 convolution_multiply_fusion.1
  57.3 0.3 copy.46
  57.6 0.3 fusion.92
  57.9 0.3 multiply_reduce_fusion
  58.2 0.3 fusion.63
  58.5 1.1 fusion.61
  59.7 0.3 copy.48
  60.0 1.8 copy.50
  61.8 1.8 exponential_select_fusion
  63.7 1.3 copy.47
  65.0 1.4 broadcast_multiply_fusion
  66.3 2.9 %copy.49 = f32[16,32,8,16]{0,3,2,1:T(8,128)} copy(f32[16,32,8,16]{1,3,2,0:T(8,128)S(1)} %broadcast_multiply_fusion) | data formatting | bytes 524288 | tf_op jit(solution)/shard_map/mul | solution.py:91
  69.3 4.8 %convolution_convert_fusion = bf16[32,8,16,16]{3,2,1,0:T(8,128)(2,1)} fusion(f32[16,32,8,16]{0,3,2,1:T(8,128)} %copy.49, f32[16,32,8,16]{3,0,2,1:T(8,128)S(1)} %copy.50), kind=kOutput, calls=%fused_computation.1 | convolution fusion | flops 12648448 | bytes 655360 | tf_op jit(solution)/shard_map/ijhe,ijhf->jhef/dot_general | solution.py:92
  74.2 0.7 broadcast_compare_fusion
  74.8 1.3 copy.51
  76.1 1.8 copy.53
  77.9 75.7 %all-reduce.5.cloned.1.call-done = bf16[32,8,16,16]{3,2,1,0:T(8,128)(2,1)} async-done(((bf16[32,8,16,16]{3,2,1,0:T(8,128)(2,1)}), bf16[32,8,16,16]{3,2,1,0:T(8,128)(2,1)}) %all-reduce.5.cloned.1.call-update) | async-done | bytes 131088 | tf_op jit(solution)/shard_map/psum | solution.py:93
  153.5 4.4 %convolution_multiply_fusion = f32[32,8,16,16]{3,2,1,0:T(8,128)} fusion(bf16[32,8,16,16]{3,2,1,0:T(8,128)(2,1)} %all-reduce.5.cloned.1.call-done, f32[16,32,8,16]{3,0,2,1:T(8,128)S(1)} %copy.53), kind=kOutput, calls=%fused_computation | convolution fusion | flops 12648448 | bytes 655360 | tf_op jit(solution)/shard_map/ijhe,jhef->ijhf/dot_general | solution.py:97
  158.0 2.3 %copy.55 = f32[16,32,128]{2,1,0:T(8,128)S(1)} copy(f32[16,32,128]{0,2,1:T(8,128)} %bitcast.87) | data formatting | bytes 524288 | tf_op jit(solution)/shard_map/reshape | solution.py:48
  160.4 0.3 convert_reduce_fusion.1
  160.7 0.3 fusion.36
  161.0 0.4 fusion.3
  161.4 0.7 reshape.216
  162.1 3.2 %all-to-all-start = ((bf16[4,2,1024]{2,1,0:T(2,128)(2,1)}), bf16[4,2,1024]{2,1,0:T(2,128)(2,1)S(1)}, u32[]{:S(2)}, u32[]{:S(2)}) async-start(bf16[4,2,1024]{2,1,0:T(2,128)(2,1)} %reshape.216), calls=%async_computation | async-start | bytes 32768 | tf_op jit(solution)/shard_map/all_to_all | solution.py:104
  165.4 30.5 %all_gather.6 = bf16[128,192]{1,0:T(8,128)(2,1)S(1)} all-gather(bf16[16,192]{1,0:T(8,128)(2,1)S(1)} %convolution_convert_fusion.6), channel_id=1, replica_groups=mesh['grp'=1,'row'=8,'col'=4] {'row'}, dimensions={0}, use_global_device_ids=true | all-gather | bytes 55296 | tf_op jit(solution)/shard_map/all_gather | solution.py:121
  196.4 0.2 fusion.93
  196.9 0.4 convolution_convert_fusion.3
  197.3 0.8 copy.66
  198.2 20.0 %reduce-scatter.4.cloned.1.call-done = bf16[192,16]{1,0:T(8,128)(2,1)} async-done(((bf16[768,16]{1,0:T(8,128)(2,1)}), bf16[192,16]{1,0:T(8,128)(2,1)}) %reduce-scatter.4.cloned.1.call-update) | async-done | bytes 6160
  218.1 1.5 copy.67
  (94 shorter events, 1.6 us)
Async XLA Ops:
  7.2 189.7 %copy-start = (bf16[192,768]{1,0:T(8,128)(2,1)S(1)}, bf16[192,768]{1,0:T(8,128)(2,1)}, u32[]{:S(2)}) copy-start(bf16[192,768]{1,0:T(8,128)(2,1)} %param.33) | copy-start | bytes 884740
  7.2 6.2 %copy-start.3 = (bf16[16,32,128]{2,1,0:T(8,128)(2,1)S(1)}, bf16[16,32,128]{2,1,0:T(8,128)(2,1)}, u32[]{:S(2)}) copy-start(bf16[16,32,128]{2,1,0:T(8,128)(2,1)} %param.17) | copy-start | bytes 393220
  7.2 6.2 %copy-start.9 = (bf16[2,128,256]{2,1,0:T(8,128)(2,1)S(1)}, bf16[2,128,256]{2,1,0:T(8,128)(2,1)}, u32[]{:S(2)}) copy-start(bf16[2,128,256]{2,1,0:T(8,128)(2,1)} %param.24) | copy-start | bytes 393220
  7.2 48.3 %all-reduce.3.cloned.1.call-start = ((), (), s32[]{:S(2)}) async-start(), calls=%async_computation.2 | async-start | bytes 1048576 | tf_op jit(solution)/shard_map/psum | solution.py:86
  8.0 13.1 %copy-start.29 = (f32[128]{0:T(128)}, f32[128]{0:T(128)S(1)}, u32[]{:S(2)}) copy-start(f32[128]{0:T(128)S(1)} %convert_element_type.100) | copy-start | bytes 1540
  13.8 3.2 %copy-start.7 = (bf16[16,768]{1,0:T(8,128)(2,1)S(1)}, bf16[16,768]{1,0:T(8,128)(2,1)}, u32[]{:S(2)}) copy-start(bf16[16,768]{1,0:T(8,128)(2,1)} %param.18) | copy-start | bytes 73732
  13.8 3.5 %copy-start.12 = (f32[768]{0:T(1024)S(1)}, f32[768]{0:T(1024)}, u32[]{:S(2)}) copy-start(f32[768]{0:T(1024)} %param.30) | copy-start | bytes 9220
  14.2 6.7 %copy-start.19 = (s32[128]{0:T(128)S(1)}, s32[128]{0:T(128)}, u32[]{:S(2)}) copy-start(s32[128]{0:T(128)} %param.21) | copy-start | bytes 1540
  14.2 7.4 %copy-start.6 = (f32[16,32,128]{2,1,0:T(8,128)S(1)}, f32[16,32,128]{2,1,0:T(8,128)}, u32[]{:S(2)}) copy-start(f32[16,32,128]{2,1,0:T(8,128)} %get-tuple-element.4) | copy-start | bytes 786436
  16.8 38.0 %copy-start.20 = (s32[128]{0:T(128)S(1)}, s32[128]{0:T(128)}, u32[]{:S(2)}) copy-start(s32[128]{0:T(128)} %param.20) | copy-start | bytes 1540
  16.9 136.7 %all-reduce.5.cloned.1.call-start = ((), (), s32[]{:S(2)}) async-start(), calls=%async_computation.3 | async-start | bytes 2097152 | tf_op jit(solution)/shard_map/psum | solution.py:93
  17.1 3.8 %copy-start.13 = (f32[16]{0:T(128)}, f32[16]{0:T(128)S(1)}, u32[]{:S(2)}) copy-start(f32[16]{0:T(128)S(1)} %broadcast_multiply_fusion.4) | copy-start | bytes 196
  17.3 3.6 %copy-start.16 = (f32[16]{0:T(128)}, f32[16]{0:T(128)S(1)}, u32[]{:S(2)}) copy-start(f32[16]{0:T(128)S(1)} %add_rsqrt_fusion.3) | copy-start | bytes 196
  22.0 35.6 %copy-start.23 = (bf16[2,128,128]{2,1,0:T(8,128)(2,1)S(1)}, bf16[2,128,128]{2,1,0:T(8,128)(2,1)}, u32[]{:S(2)}) copy-start(bf16[2,128,128]{2,1,0:T(8,128)(2,1)} %param.25) | copy-start | bytes 196612
  57.3 1.2 copy-start.10
  57.9 1.8 copy-start.1
  58.5 1.1 copy-start.4
  60.0 4.9 %copy-start.18 = (f32[16]{0:T(128)S(1)}, f32[16]{0:T(128)}, u32[]{:S(2)}) copy-start(f32[16]{0:T(128)} %dynamic_slice.13) | copy-start | bytes 196
  69.3 4.9 %copy-start.21 = (s32[128]{0:T(128)S(1)}, s32[128]{0:T(128)}, u32[]{:S(2)}) copy-start(s32[128]{0:T(128)} %param.20) | copy-start | bytes 1540
  69.3 4.9 %copy-start.22 = (s32[16]{0:T(128)S(1)}, s32[16]{0:T(128)}, u32[]{:S(2)}) copy-start(s32[16]{0:T(128)} %dynamic_slice.14) | copy-start | bytes 196
  158.0 2.3 %copy-start.2 = (f32[16,32,128]{2,1,0:T(8,128)S(1)}, f32[16,32,128]{2,1,0:T(8,128)}, u32[]{:S(2)}) copy-start(f32[16,32,128]{2,1,0:T(8,128)} %copy-done.1) | copy-start | bytes 786436
  158.0 2.4 %copy-start.5 = (f32[16,32,256]{2,1,0:T(8,128)S(1)}, f32[16,32,256]{2,1,0:T(8,128)}, u32[]{:S(2)}) copy-start(f32[16,32,256]{2,1,0:T(8,128)} %copy-done.4) | copy-start | bytes 1572868
  158.0 2.4 %copy-start.24 = (bf16[2,128,128]{2,1,0:T(8,128)(2,1)S(1)}, bf16[2,128,128]{2,1,0:T(8,128)(2,1)}, u32[]{:S(2)}) copy-start(bf16[2,128,128]{2,1,0:T(8,128)(2,1)} %param.25) | copy-start | bytes 196612
  158.0 3.0 %copy-start.25 = (bf16[128,16]{0,1:T(8,128)(2,1)S(1)}, bf16[128,16]{0,1:T(8,128)(2,1)}, u32[]{:S(2)}) copy-start(bf16[128,16]{0,1:T(8,128)(2,1)} %param.27) | copy-start | bytes 12292
  158.0 3.0 %copy-start.26 = (f32[128]{0:T(128)S(1)}, f32[128]{0:T(128)}, u32[]{:S(2)}) copy-start(f32[128]{0:T(128)} %param.26) | copy-start | bytes 1540
  158.0 38.4 %copy-start.15 = (pred[16,128]{1,0:T(8,128)(4,1)S(1)}, pred[16,128]{1,0:T(8,128)(4,1)}, u32[]{:S(2)}) copy-start(pred[16,128]{1,0:T(8,128)(4,1)} %broadcast_compare_fusion) | copy-start | bytes 6148
  158.0 38.3 %copy-start.27 = (f32[4]{0:T(128)S(1)}, f32[4]{0:T(128)}, u32[]{:S(2)}) copy-start(f32[4]{0:T(128)} %param.29) | copy-start | bytes 52
  158.0 38.3 %copy-start.28 = (f32[4]{0:T(128)S(1)}, f32[4]{0:T(128)}, u32[]{:S(2)}) copy-start(f32[4]{0:T(128)} %param.28) | copy-start | bytes 52
  158.0 38.3 %copy-start.30 = (f32[128]{0:T(128)S(1)}, f32[128]{0:T(128)}, u32[]{:S(2)}) copy-start(f32[128]{0:T(128)} %copy-done.29) | copy-start | bytes 1540
  160.3 36.5 %copy-start.8 = (bf16[2,768,192]{1,2,0:T(8,128)(2,1)S(1)}, bf16[2,768,192]{1,2,0:T(8,128)(2,1)}, u32[]{:S(2)}) copy-start(bf16[2,768,192]{1,2,0:T(8,128)(2,1)} %param.32) | copy-start | bytes 1769476
  160.3 36.5 %copy-start.14 = (f32[16]{0:T(128)S(1)}, f32[16]{0:T(128)}, u32[]{:S(2)}) copy-start(f32[16]{0:T(128)} %copy-done.13) | copy-start | bytes 196
  160.4 36.5 %copy-start.17 = (f32[16]{0:T(128)S(1)}, f32[16]{0:T(128)}, u32[]{:S(2)}) copy-start(f32[16]{0:T(128)} %copy-done.16) | copy-start | bytes 196
  160.7 59.0 %copy-start.11 = (bf16[16,32,128]{2,1,0:T(8,128)(2,1)}, bf16[16,32,128]{2,1,0:T(8,128)(2,1)S(1)}, u32[]{:S(2)}) copy-start(bf16[16,32,128]{2,1,0:T(8,128)(2,1)S(1)} %get-tuple-element.11) | copy-start | bytes 393220
  162.1 33.9 %all-to-all-start = ((bf16[4,2,1024]{2,1,0:T(2,128)(2,1)}), bf16[4,2,1024]{2,1,0:T(2,128)(2,1)S(1)}, u32[]{:S(2)}, u32[]{:S(2)}) async-start(bf16[4,2,1024]{2,1,0:T(2,128)(2,1)} %reshape.216), calls=%async_computation | async-start | bytes 32768 | tf_op jit(solution)/shard_map/all_to_all | solution.py:104
  165.3 52.8 %reduce-scatter.4.cloned.1.call-start = ((), (), s32[]{:S(2)}) async-start(), calls=%async_computation.4 | async-start | bytes 245760
Sparse Core Ops, SparseCore 0:
  17.0 36.1 all-reduce.2
  74.3 79.2 all-reduce.4
  198.3 19.8 reduce-scatter.3
where the time goes:
time: 227 us; the launch traced here: 226 us
  waiting for transfers between devices  95.7 us (42%)
  blocking collectives  63.2 us (28%)
  matrix products  21.9 us (10%)
  local copies, waits for them, and re-layouts  19 us (8%)
  between operations  14.4 us (6%)
  other arithmetic  8.56 us (4%)
  starting transfers between devices  3.36 us (1%)
    psum x1, waiting for transfers between devices, on_device(): lax.psum(col_sums.reshape(col_count, -1).astype(jnp.bfloat16), 'row')  75.7 us
    all_gather x1, blocking collectives, on_device(): piece_keys = lax.all_gather(key_rows, 'row', axis=0, tiled=True)  32.7 us
    all_gather x1, blocking collectives, on_device(): piece_values = lax.all_gather(value_rows, 'row', axis=0, tiled=True)  30.5 us
    unnamed x4, waiting for transfers between devices  20 us
    select_n x5, local copies, waits for them, and re-layouts, feature(): jnp.where(inputs > 0, inputs + 1.0, jnp.exp(jnp.minimum(inputs, 0.0)))  5.04 us
    dot_general x1, matrix products, on_device(): jnp.einsum('ijhe,ijhf->jhef', key_feat, values, precision=highest)  4.84 us
  transfers between devices with their start and end apart: 4, of which 2 were waited for; matrix products, arithmetic and copies ran while one was open for 4% of the time, Pallas kernels for 0%

commit v1 on v0

v1 whole, which is shorter than its diff:
```python
import functools
import math

import jax
import jax.numpy as jnp
from jax import lax
from jax.experimental import pallas as pl
from jax.experimental.pallas import tpu as pltpu
from jax.sharding import PartitionSpec as P

C = 128
TRI_HEADS = 8
TRI_DIM = 16
HEAD_DIM = 48
PAD_ROWS = 8

epsilon = 1e-05
cap_value = 10.0
rel_reach = 32.0

F32 = jnp.float32
BF16 = jnp.bfloat16
VMEM = pl.BlockSpec(memory_space=pltpu.VMEM)
SMEM = pl.BlockSpec(memory_space=pltpu.SMEM)


def mm(a, b):
    return jnp.dot(a, b, preferred_element_type=F32)


def mm_nt(a, b):
    return lax.dot_general(a, b, (((1,), (1,)), ((), ())), preferred_element_type=F32)


def mm_tn(a, b):
    return lax.dot_general(a, b, (((0,), (0,)), ((), ())), preferred_element_type=F32)


def iota(shape, dim):
    return lax.broadcasted_iota(jnp.int32, shape, dim)


def layer_norm(x, gain):
    centered = x - jnp.mean(x, -1, keepdims=True)
    spread = jnp.mean(centered * centered, -1, keepdims=True)
    return centered * lax.rsqrt(spread + epsilon) * gain


def feature(x):
    return jnp.where(x > 0, x + 1.0, jnp.exp(jnp.minimum(x, 0.0)))


def sigmoid(x):
    return 1.0 / (1.0 + jnp.exp(-x))


def triangle(x, lines, length, gain, qk, vg, out, scale):
    tokens = x.shape[0] // lines
    normed = layer_norm(x, gain).astype(BF16)
    query_key = mm(normed, qk)
    value_gate = mm(normed, vg)
    valid = iota((tokens, C), 0) < length
    same_head = (iota((C, C), 0) // TRI_DIM) == (iota((C, C), 1) // TRI_DIM)
    lines_out = []
    for line in range(lines):
        rows = slice(line * tokens, (line + 1) * tokens)
        query = feature(query_key[rows, :C]).astype(BF16)
        key = jnp.where(valid, feature(query_key[rows, C:]), 0.0).astype(BF16)
        values = value_gate[rows, :C].astype(BF16)
        state = jnp.where(same_head, mm_tn(key, values) * scale, 0.0).astype(BF16)
        update = (sigmoid(value_gate[rows, C:]) * mm(query, state)).astype(BF16)
        lines_out.append(x[rows] + mm(update, out))
    return lines_out


def row_kernel(scale, n_col, lines, me_ref, mask_ref, gain_ref, qk_ref, vg_ref, out_w_ref, *refs):
    pieces, z_ref, x_scr, z_scr = refs[:n_col], refs[n_col], refs[n_col + 1], refs[n_col + 2]
    block = pieces[0].shape[0] // lines
    tokens = block * n_col
    me = me_ref[0]
    for k in range(n_col):
        source = me ^ k
        for line in range(lines):
            start = pl.multiple_of(line * tokens + source * block, block)
            x_scr[pl.ds(start, block), :] = pieces[k][line * block : (line + 1) * block, :].astype(F32)
    length = jnp.sum(mask_ref[...])
    done = triangle(
        x_scr[...], lines, length, gain_ref[0:1, :], qk_ref[0], vg_ref[0], out_w_ref[0], scale
    )
    for line in range(lines):
        z_scr[line * tokens : (line + 1) * tokens, :] = done[line]
    owners, per_owner, _ = z_ref.shape
    for d in range(owners):
        z_ref[d] = z_scr[pl.ds(d, per_owner, stride=owners), :].astype(BF16)


def col_kernel(
    scale, n_row, n_col, row_count, col_count, heads_here,
    mask_ref, gain_ref, qk_ref, vg_ref, out_w_ref, bias_gain_ref, bias_proj_ref, z_ref, out_ref, z_scr,
):
    lines = z_scr.shape[0] // (n_row * row_count)
    tokens = n_row * row_count
    devices = n_row * n_col
    z_scr[...] = z_ref[...].astype(F32)
    x = jnp.concatenate([z_scr[pl.ds(line, tokens, stride=lines), :] for line in range(lines)], axis=0)
    length = jnp.sum(mask_ref[...])
    done = triangle(x, lines, length, gain_ref[1:2, :], qk_ref[1], vg_ref[1], out_w_ref[1], scale)
    done = [part.astype(BF16) for part in done]
    normed = [layer_norm(part.astype(F32), bias_gain_ref[...]).astype(BF16) for part in done]
    width = lines * row_count
    for r in range(n_row):
        rows = slice(r * row_count, (r + 1) * row_count)
        bias = mm_nt(bias_proj_ref[...], jnp.concatenate([part[rows] for part in normed], axis=0))
        for c in range(n_col):
            dest = r * n_col + c
            out_ref[dest, :row_count, :] = done[c * col_count // devices][rows]
            out_ref[dest, row_count:, :] = jnp.zeros((PAD_ROWS, C), BF16)
            out_ref[dest, row_count : row_count + heads_here, :width] = bias[
                c * heads_here : (c + 1) * heads_here, :
            ].astype(BF16)


def token_kernel(single_ref, gain_ref, qk_ref, vg_ref, q_ref, kv_ref, g_ref):
    width = q_ref.shape[1]
    normed = layer_norm(single_ref[...].astype(F32), gain_ref[...]).astype(BF16)
    q_ref[...] = mm_nt(normed, qk_ref[0]).astype(BF16)
    kv_ref[0] = mm_nt(normed, qk_ref[1]).astype(BF16)
    kv_ref[1] = mm_nt(normed, vg_ref[0]).astype(BF16)
    g_ref[...] = mm_nt(normed, vg_ref[1])


def attn_kernel(
    n_row, n_col, row_count, heads_here,
    me_ref, chain_bias_ref, slope_ref, mask_ref, chain_ref, residue_ref, q_ref, g_ref, out_w_ref, got_ref, *refs,
):
    kv_refs, o_ref, k_scr, v_scr = refs[:-3], refs[-3], refs[-2], refs[-1]
    tokens = n_row * row_count
    devices = n_row * n_col
    lines = tokens // devices
    width = heads_here * HEAD_DIM
    me = me_ref[0]
    slot = 0
    for ref in kv_refs:
        for t in range(ref.shape[0]):
            start = pl.multiple_of((me ^ slot) * row_count, row_count)
            k_scr[pl.ds(start, row_count), :] = ref[t, 0].astype(F32)
            v_scr[pl.ds(start, row_count), :] = ref[t, 1].astype(F32)
            slot += 1
    keys, values = k_scr[...].astype(BF16), v_scr[...].astype(BF16)

    own = iota((row_count, tokens), 1) == iota((row_count, tokens), 0) + me * row_count
    chain = chain_ref[...].astype(F32)
    residue = residue_ref[...].astype(F32)
    my_chain = jnp.sum(jnp.where(own, chain, 0.0), -1, keepdims=True)
    my_residue = jnp.sum(jnp.where(own, residue, 0.0), -1, keepdims=True)
    same_chain = my_chain == chain
    offset = jnp.clip(my_residue - residue, -rel_reach, rel_reach) / rel_reach
    length = jnp.sum(mask_ref[...])
    valid = iota((row_count, tokens), 1) < length

    count = devices * PAD_ROWS
    got = got_ref[:, row_count:, :].astype(F32).reshape(count, C).astype(BF16)
    src, dst = iota((count, heads_here * devices), 0), iota((count, heads_here * devices), 1)
    place = ((src % PAD_ROWS == dst // devices) & (src // PAD_ROWS == dst % devices)).astype(F32).astype(BF16)
    turned = mm_tn(got, place)

    head_of = iota((row_count, width), 1) // HEAD_DIM
    query = q_ref[...].astype(F32)
    stacked = jnp.concatenate(
        [jnp.where(head_of == h, query, 0.0) for h in range(heads_here)], axis=0
    ).astype(BF16)
    scores = mm_nt(stacked, keys) / math.sqrt(HEAD_DIM)
    weights = []
    for h in range(heads_here):
        bias = jnp.concatenate(
            [
                turned[line * row_count : (line + 1) * row_count, h * devices : (h + 1) * devices]
                for line in range(lines)
            ],
            axis=1,
        )
        e = scores[h * row_count : (h + 1) * row_count] + bias
        e = e + jnp.where(same_chain, chain_bias_ref[h] + slope_ref[h] * offset, 0.0)
        weights.append(jnp.where(valid, jnp.exp(cap_value * jnp.tanh(e / cap_value)), 0.0))
    numerator = mm(jnp.concatenate(weights, axis=0).astype(BF16), values)
    attended = jnp.zeros((row_count, width), F32)
    for h in range(heads_here):
        part = numerator[h * row_count : (h + 1) * row_count] / jnp.sum(weights[h], -1, keepdims=True)
        attended = jnp.where(head_of == h, part, attended)
    gated = (sigmoid(g_ref[...]) * attended).astype(BF16)
    full = mm(gated, out_w_ref[...])
    share = full.shape[1] // n_col
    for c in range(n_col):
        o_ref[c] = full[:, c * share : (c + 1) * share].astype(BF16)


def pair_kernel(row_count, got_ref, out_ref, scr):
    sources = got_ref.shape[0]
    scr[...] = got_ref[:, :row_count, :].astype(F32).reshape(sources * row_count, C)
    for i in range(row_count):
        out_ref[i] = scr[pl.ds(i, sources, stride=row_count), :].astype(BF16)


def swap_col(blocks, me, n_col):
    pieces = []
    for k in range(n_col):
        piece = lax.dynamic_index_in_dim(blocks, me ^ k, 0, keepdims=False)
        if k:
            piece = lax.ppermute(piece, "col", [(i, i ^ k) for i in range(n_col)])
        pieces.append(piece)
    return pieces


def on_device(
    n_row, n_col,
    pair_act, single, token_mask, chain_index, residue_index, tri_gain, tri_qk, tri_vg, tri_out,
    bias_gain, bias_proj, chain_bias, pos_slope, attn_gain, attn_qk, attn_vg, attn_out,
):
    tokens = token_mask.shape[0]
    row_count, col_count = pair_act.shape[0], pair_act.shape[1]
    heads_here = chain_bias.shape[0]
    devices = n_row * n_col
    own_rows, own_cols = row_count // n_col, tokens // devices
    scale = 1.0 / (2.0 * TRI_DIM * math.sqrt(tokens))
    my_row, my_col = lax.axis_index("row"), lax.axis_index("col")
    row_id, col_id = my_row.reshape(1), my_col.reshape(1)
    mask2 = token_mask.reshape(1, tokens)
    width = heads_here * HEAD_DIM

    pieces = swap_col(pair_act.reshape(n_col, own_rows * col_count, C), my_col, n_col)
    per_owner = own_rows * own_cols
    z_out = pl.pallas_call(
        functools.partial(row_kernel, scale, n_col, own_rows),
        out_shape=jax.ShapeDtypeStruct((devices, per_owner, C), BF16),
        in_specs=[SMEM] + [VMEM] * (5 + n_col),
        out_specs=VMEM,
        scratch_shapes=[pltpu.VMEM((own_rows * tokens, C), F32)] * 2,
        name="row_pass",
    )(col_id, mask2, tri_gain, tri_qk, tri_vg, tri_out, *pieces)

    z_in = lax.all_to_all(z_out, ("row", "col"), 0, 0, tiled=True)
    back = pl.pallas_call(
        functools.partial(col_kernel, scale, n_row, n_col, row_count, col_count, heads_here),
        out_shape=jax.ShapeDtypeStruct((devices, row_count + PAD_ROWS, C), BF16),
        in_specs=[VMEM] * 8,
        out_specs=VMEM,
        scratch_shapes=[pltpu.VMEM((own_cols * tokens, C), F32)],
        name="col_pass",
    )(
        mask2, tri_gain, tri_qk, tri_vg, tri_out, bias_gain.reshape(1, C), bias_proj.T,
        z_in.reshape(own_cols * tokens, C),
    )
    got = lax.all_to_all(back, ("row", "col"), 0, 0, tiled=True)

    query, kv, gate = pl.pallas_call(
        token_kernel,
        out_shape=(
            jax.ShapeDtypeStruct((row_count, width), BF16),
            jax.ShapeDtypeStruct((2, row_count, width), BF16),
            jax.ShapeDtypeStruct((row_count, width), F32),
        ),
        in_specs=[VMEM] * 4,
        out_specs=(VMEM,) * 3,
        name="token_proj",
    )(single, attn_gain.reshape(1, -1), attn_qk.swapaxes(1, 2), attn_vg.swapaxes(1, 2))
    held = [kv[None]]
    step = 1
    while step < n_row:
        sent = held[0] if len(held) == 1 else jnp.concatenate(held, axis=0)
        held.append(lax.ppermute(sent, "row", [(i, i ^ step) for i in range(n_row)]))
        step *= 2

    terms = pl.pallas_call(
        functools.partial(attn_kernel, n_row, n_col, row_count, heads_here),
        out_shape=jax.ShapeDtypeStruct((n_col, row_count, attn_out.shape[1] // n_col), BF16),
        in_specs=[SMEM] * 3 + [VMEM] * (7 + len(held)),
        out_specs=VMEM,
        scratch_shapes=[pltpu.VMEM((tokens, width), F32)] * 2,
        name="token_attention",
    )(
        row_id, chain_bias, pos_slope, mask2, chain_index.reshape(1, tokens), residue_index.reshape(1, tokens),
        query, gate, attn_out, got, *held,
    )
    parts = swap_col(terms, my_col, n_col)
    token_update = sum(part.astype(F32) for part in parts).astype(BF16)

    first = my_col * col_count % devices
    mine = got if col_count == devices else lax.dynamic_slice_in_dim(got, first, col_count, 0)
    pair_out = pl.pallas_call(
        functools.partial(pair_kernel, row_count),
        out_shape=jax.ShapeDtypeStruct((row_count, col_count, C), BF16),
        in_specs=[VMEM],
        out_specs=VMEM,
        scratch_shapes=[pltpu.VMEM((col_count * row_count, C), F32)],
        name="pair_order",
    )(mine)
    return (pair_out, token_update)


def solution(mesh):
    return jax.shard_map(
        functools.partial(on_device, mesh.shape["row"], mesh.shape["col"]),
        mesh=mesh,
        in_specs=(
            P(("grp", "row"), "col", None),
            P(("grp", "row"), None),
            P("grp"),
            P("grp"),
            P("grp"),
            P(),
            P(),
            P(),
            P(),
            P(),
            P(),
            P("col"),
            P("col"),
            P(),
            P(None, None, "col"),
            P(None, None, "col"),
            P("col", None),
        ),
        out_specs=(P(("grp", "row"), "col", None), P(("grp", "row"), "col")),
        check_vma=False,
    )
```

time: 227 us -> 60.1 us (0.26)
  waiting for transfers between devices: 95.7 us -> 11.7 us
  blocking collectives: 63.2 us -> 13.6 us
  matrix products: 21.9 us -> 0 us
  local copies, waits for them, and re-layouts: 19 us -> 4.65 us
  between operations: 14.4 us -> 0.7 us
  Pallas kernels: 0 us -> 13.2 us
  starting transfers between devices: 3.36 us -> 13.6 us
  other arithmetic: 8.56 us -> 2.05 us
    psum x2 -> x0, waiting for transfers between devices: 75.7 us -> none  [the longest x1 75.7 us: on_device(): lax.psum(col_sums.reshape(col_count, -1).astype(jnp.bfloat16), 'row')]
    all_gather x2 -> x0, blocking collectives: 63.2 us -> none  [the longest x1 32.7 us: on_device(): piece_keys = lax.all_gather(key_rows, 'row', axis=0, tiled=True)]
    dot_general x17 -> x0, matrix products: 21.9 us -> none  [the longest x1 4.84 us: on_device(): jnp.einsum('ijhe,ijhf->jhef', key_feat, values, precision=highest)]
    unnamed x4 -> x0, waiting for transfers between devices: 20 us -> none
    all_to_all x0 -> x1, blocking collectives: none -> 13.6 us  [on_device(): z_in = lax.all_to_all(z_out, ('row', 'col'), 0, 0, tiled=True)]
    pallas_call x0 -> x5, Pallas kernels: none -> 13.2 us  [the longest x1 3.53 us: on_device(): pl.pallas_call(functools.partial(col_kernel, scale, n_row, n_col, row_cou...]
    ppermute x0 -> x9, waiting for transfers between devices: none -> 11.7 us  [the longest x3 7.27 us: on_device(): lax.ppermute(sent, 'row', [(i, i ^ step) for i in range(n_row)])]
    ppermute x0 -> x9, starting transfers between devices: none -> 10.9 us  [the longest x3 5.94 us: on_device(): lax.ppermute(sent, 'row', [(i, i ^ step) for i in range(n_row)])]
  transfers between devices with their start and end apart: 4 -> 10, of which waited for: 2 -> 7; matrix products, arithmetic and copies ran while one was open for 4% -> 2% of each run, Pallas kernels for 0% -> 7%
where the time goes in v1:
time: 60.1 us; the launch traced here: 59.5 us
  starting transfers between devices  13.6 us (23%)
  blocking collectives  13.6 us (23%)
  Pallas kernels  13.2 us (22%)
  waiting for transfers between devices  11.7 us (19%)
  local copies, waits for them, and re-layouts  4.65 us (8%)
  other arithmetic  2.05 us (3%)
  between operations  0.7 us (1%)
    all_to_all x1, blocking collectives, on_device(): z_in = lax.all_to_all(z_out, ('row', 'col'), 0, 0, tiled=True)  13.6 us
    ppermute x3, waiting for transfers between devices, on_device(): lax.ppermute(sent, 'row', [(i, i ^ step) for i in range(n_row)])  7.27 us
    ppermute x3, starting transfers between devices, on_device(): lax.ppermute(sent, 'row', [(i, i ^ step) for i in range(n_row)])  5.94 us
    ppermute x6, starting transfers between devices, swap_col(): piece = lax.ppermute(piece, 'col', [(i, i ^ k) for i in range(n_col)])  4.94 us
    ppermute x6, waiting for transfers between devices, swap_col(): piece = lax.ppermute(piece, 'col', [(i, i ^ k) for i in range(n_col)])  4.44 us
    pallas_call x1, Pallas kernels, on_device(): pl.pallas_call(functools.partial(col_kernel, scale, n_row, n_col, row_cou...  3.53 us
    pallas_call x1, Pallas kernels, on_device(): pl.pallas_call(functools.partial(row_kernel, scale, n_col, own_rows), out...  3.16 us
    all_to_all x1, starting transfers between devices, on_device(): got = lax.all_to_all(back, ('row', 'col'), 0, 0, tiled=True)  2.71 us
  transfers between devices with their start and end apart: 10, of which 7 were waited for; matrix products, arithmetic and copies ran while one was open for 2% of the time, Pallas kernels for 7%

profile of v1, /device:TPU:0, one launch (start us, length us, event | category | flops | bytes accessed | tf_op | source)
XLA Modules:
  0.0 59.5 jit_solution(283587848595567494)
XLA Ops:
  0.6 1.4 %dynamic-slice_bitcast_fusion = (bf16[128,128]{1,0:T(8,128)(2,1)S(1)}, bf16[128,128]{1,0:T(8,128)(2,1)S(1)}, bf16[128,128]{1,0:T(8,128)(2,1)S(1)}, bf16[128,128]{1,0:T(8,128)(2,1)}) fusion(bf16[4,128,128]{2,1,0:T(8,128)(2,1)} %bitcast.36, s32[]{:T(128)S(6)} %select_n.21, s32[]{:T(128)S(6)} %select_n.20, s32[]{:T(128)S(6)} %select_n.19, s32[]{:T(128)S(6)} %select_n.18), kind=kLoop, calls=%fused_computation.2 | loop fusion | bytes 262160 | tf_op jit(solution)/shard_map/jit(dynamic_index_in_dim)/squeeze | solution.py:207
  2.1 0.5 collective-permute-start
  2.6 2.5 %collective-permute-start.1 = (bf16[128,128]{1,0:T(8,128)(2,1)S(1)}, bf16[128,128]{1,0:T(8,128)(2,1)S(1)}, u32[]{:S(2)}, u32[]{:S(2)}) collective-permute-start(bf16[128,128]{1,0:T(8,128)(2,1)S(1)} %get-tuple-element.9), channel_id=1, source_target_pairs={{0,2},{1,3},{2,0},{3,1},{4,6},{5,7},{6,4},{7,5},{8,10},{9,11},{10,... | collective-permute-start | bytes 98312 | tf_op jit(solution)/shard_map/ppermute | solution.py:209
  5.1 0.1 collective-permute-start.2
  5.2 0.0 collective-permute-done.refs_1_
  5.2 0.0 copy-start.5
  5.2 1.9 %collective-permute-done.1.refs_2_ = bf16[128,128]{1,0:T(8,128)(2,1)S(1)} collective-permute-done((bf16[128,128]{1,0:T(8,128)(2,1)S(1)}, bf16[128,128]{1,0:T(8,128)(2,1)S(1)}, u32[]{:S(2)}, u32[]{:S(2)}) %collective-permute-start.1) | collective-permute-done | bytes 32800 | tf_op jit(solution)/shard_map/ppermute | solution.py:209
  7.1 0.0 copy-start.6
  7.1 1.3 %collective-permute-done.2.refs_3_ = bf16[128,128]{1,0:T(8,128)(2,1)S(1)} collective-permute-done((bf16[128,128]{1,0:T(8,128)(2,1)S(1)}, bf16[128,128]{1,0:T(8,128)(2,1)S(1)}, u32[]{:S(2)}, u32[]{:S(2)}) %collective-permute-start.2) | collective-permute-done | bytes 32800 | tf_op jit(solution)/shard_map/ppermute | solution.py:209
  8.4 0.0 copy-start.7
  8.4 0.0 copy-done.5
  8.4 0.0 copy-done.6
  8.4 0.6 %copy-done.7 = bf16[128,128]{1,0:T(8,128)(2,1)} copy-done((bf16[128,128]{1,0:T(8,128)(2,1)}, bf16[128,128]{1,0:T(8,128)(2,1)S(1)}, u32[]{:S(2)}) %copy-start.7) | copy-done | bytes 32792
  9.0 3.2 %row_pass.1 = bf16[32,16,128]{2,1,0:T(8,128)(2,1)} custom-call(s32[1]{0:T(128)} %bitcast.3.me_ref, s32[1,128]{1,0:T(1,128)} %bitcast.37, f32[2,128]{1,0:T(2,128)} %gain_ref.3, bf16[2,128,256]{2,1,0:T(8,128)(2,1)} %qk_ref.3, bf16[2,128,256]{2,1,0:T(8,128)(2,1)} %vg_ref.3, bf16[2,128,128]{2,1,0:T(8,128)(2,1)} %out_w_ref.4, ...), custom_call_target="tpu_custom_call" | custom-call | tf_op jit(solution)/shard_map/row_pass/pallas_call | solution.py:232
  12.2 13.6 %all_to_all.10 = bf16[32,16,128]{2,1,0:T(8,128)(2,1)} all-to-all(bf16[32,16,128]{2,1,0:T(8,128)(2,1)} %row_pass.1), channel_id=1, replica_groups=mesh['grp'=1,'row'=8,'col'=4] {'row','col'}, dimensions={0} | all-to-all | bytes 262144 | tf_op jit(solution)/shard_map/all_to_all | solution.py:241
  25.8 3.5 %col_pass.1 = bf16[32,24,128]{2,1,0:T(8,128)(2,1)} custom-call(s32[1,128]{1,0:T(1,128)} %bitcast.38, f32[2,128]{1,0:T(2,128)} %gain_ref.3, bf16[2,128,256]{2,1,0:T(8,128)(2,1)} %qk_ref.3, bf16[2,128,256]{2,1,0:T(8,128)(2,1)} %vg_ref.3, bf16[2,128,128]{2,1,0:T(8,128)(2,1)} %out_w_ref.4, f32[1,128]{1,0:T(1,128)} %bitcast.41, bf16[16,128]{1,0:T(8,128)(2,1)} %bitcast.40, ...), custom_call_target="tpu_custom_call" | custom-call | tf_op jit(solution)/shard_map/col_pass/pallas_call | solution.py:242
  29.3 0.0 copy-start.8
  29.3 2.7 %all-to-all-start.1 = ((bf16[32,24,128]{2,1,0:T(8,128)(2,1)}), bf16[32,24,128]{2,1,0:T(8,128)(2,1)S(1)}, u32[]{:S(2)}, u32[]{:S(2)}) async-start(bf16[32,24,128]{2,1,0:T(8,128)(2,1)} %col_pass.1), calls=%async_computation.1 | async-start | bytes 393216 | tf_op jit(solution)/shard_map/all_to_all | solution.py:253
  32.0 0.0 copy-done.8
  32.0 0.6 reshape.41.gain_ref
  32.6 2.4 %token_proj.1 = (bf16[16,192]{1,0:T(8,128)(2,1)}, bf16[2,16,192]{2,1,0:T(8,128)(2,1)}, f32[16,192]{1,0:T(8,128)}) custom-call(bf16[16,768]{1,0:T(8,128)(2,1)} %single_ref.1, f32[1,768]{1,0:T(1,128)} %reshape.41.gain_ref, bf16[2,192,768]{2,1,0:T(8,128)(2,1)} %bitcast.29, bf16[2,192,768]{2,1,0:T(8,128)(2,1)} %bitcast.30), custom_call_target="tpu_custom_call" | custom-call | tf_op jit(solution)/shard_map/token_proj/pallas_call | solution.py:255
  35.0 0.0 copy-start.1
  35.0 1.7 %collective-permute-start.3 = (bf16[1,2,16,192]{3,2,1,0:T(8,128)(2,1)}, bf16[1,2,16,192]{3,2,1,0:T(8,128)(2,1)S(1)}, u32[]{:S(2)}, u32[]{:S(2)}) collective-permute-start(bf16[1,2,16,192]{3,2,1,0:T(8,128)(2,1)} %bitcast.32), channel_id=1, source_target_pairs={{0,4},{4,0},{8,12},{12,8},{16,20},{20,16},{24,28},{28,24},{1,5},{5... | collective-permute-start | bytes 36872 | tf_op jit(solution)/shard_map/ppermute | solution.py:270
  36.7 2.4 %collective-permute-done.3.refs_1_ = bf16[1,2,16,192]{3,2,1,0:T(8,128)(2,1)S(1)} collective-permute-done((bf16[1,2,16,192]{3,2,1,0:T(8,128)(2,1)}, bf16[1,2,16,192]{3,2,1,0:T(8,128)(2,1)S(1)}, u32[]{:S(2)}, u32[]{:S(2)}) %collective-permute-start.3) | collective-permute-done | bytes 12320 | tf_op jit(solution)/shard_map/ppermute | solution.py:270
  39.1 0.0 copy-start.2
  39.1 0.7 %pad_maximum_fusion.1 = bf16[2,2,16,192]{3,2,1,0:T(8,128)(2,1)S(1)} fusion(bf16[1,2,16,192]{3,2,1,0:T(8,128)(2,1)S(1)} %collective-permute-done.3.refs_1_, bf16[1,2,16,192]{3,2,1,0:T(8,128)(2,1)} %bitcast.33), kind=kLoop, calls=%fused_computation.1 | loop fusion | flops 12288 | bytes 49152 | tf_op jit(solution)/shard_map/concatenate | solution.py:269
  39.8 1.7 %collective-permute-start.4 = (bf16[2,2,16,192]{3,2,1,0:T(8,128)(2,1)S(1)}, bf16[2,2,16,192]{3,2,1,0:T(8,128)(2,1)S(1)}, u32[]{:S(2)}, u32[]{:S(2)}) collective-permute-start(bf16[2,2,16,192]{3,2,1,0:T(8,128)(2,1)S(1)} %pad_maximum_fusion.1), channel_id=1, source_target_pairs={{0,8},{4,12},{8,0},{12,4},{16,24},{20,28},{24,16},{28,20},{1,9},{5... | collective-permute-start | bytes 73736 | tf_op jit(solution)/shard_map/ppermute | solution.py:270
  41.5 2.3 %collective-permute-done.4.refs_2_ = bf16[2,2,16,192]{3,2,1,0:T(8,128)(2,1)S(1)} collective-permute-done((bf16[2,2,16,192]{3,2,1,0:T(8,128)(2,1)S(1)}, bf16[2,2,16,192]{3,2,1,0:T(8,128)(2,1)S(1)}, u32[]{:S(2)}, u32[]{:S(2)}) %collective-permute-start.4) | collective-permute-done | bytes 24608 | tf_op jit(solution)/shard_map/ppermute | solution.py:270
  43.8 0.0 copy-done.2
  43.8 0.0 copy-done.1
  43.8 0.0 copy-start.3
  43.8 0.6 copy-done.3
  44.4 2.6 %collective-permute-start.5 = (bf16[4,2,16,192]{3,2,1,0:T(8,128)(2,1)S(1)}, bf16[4,2,16,192]{3,2,1,0:T(8,128)(2,1)S(1)}, u32[]{:S(2)}, u32[]{:S(2)}) collective-permute-start(bf16[4,2,16,192]{3,2,1,0:T(8,128)(2,1)S(1)} %pad_maximum_fusion), channel_id=1, source_target_pairs={{0,16},{4,20},{8,24},{12,28},{16,0},{20,4},{24,8},{28,12},{1,17},{... | collective-permute-start | bytes 147464 | tf_op jit(solution)/shard_map/ppermute | solution.py:270
  47.0 2.6 %collective-permute-done.5.refs_3_ = bf16[4,2,16,192]{3,2,1,0:T(8,128)(2,1)S(1)} collective-permute-done((bf16[4,2,16,192]{3,2,1,0:T(8,128)(2,1)S(1)}, bf16[4,2,16,192]{3,2,1,0:T(8,128)(2,1)S(1)}, u32[]{:S(2)}, u32[]{:S(2)}) %collective-permute-start.5) | collective-permute-done | bytes 49184 | tf_op jit(solution)/shard_map/ppermute | solution.py:270
  49.6 0.0 copy-start.4
  49.6 0.0 all-to-all-done.1.got_ref
  49.6 0.6 %copy-done.4 = bf16[4,2,16,192]{3,2,1,0:T(8,128)(2,1)} copy-done((bf16[4,2,16,192]{3,2,1,0:T(8,128)(2,1)}, bf16[4,2,16,192]{3,2,1,0:T(8,128)(2,1)S(1)}, u32[]{:S(2)}) %copy-start.4) | copy-done | bytes 49176
  50.2 0.1 copy-done
  50.3 2.4 %token_attention.1 = bf16[4,16,192]{2,1,0:T(8,128)(2,1)} custom-call(s32[1]{0:T(128)} %bitcast.10.me_ref, f32[4]{0:T(128)} %chain_bias_ref.1, f32[4]{0:T(128)} %slope_ref.1, s32[1,128]{1,0:T(1,128)} %bitcast.39, s32[1,128]{1,0:T(1,128)} %bitcast.42, s32[1,128]{1,0:T(1,128)} %bitcast.43, bf16[16,192]{1,0:T(8,128)(2,1)} %get-tuple-element.5.q_ref, ...), custom_call_target="tpu_custom_call" | custom-call | tf_op jit(solution)/shard_map/token_attention/pallas_call | solution.py:273
  52.7 0.7 %dynamic-slice_bitcast_fusion.6 = (bf16[16,192]{1,0:T(8,128)(2,1)S(1)}, bf16[16,192]{1,0:T(8,128)(2,1)S(1)}, bf16[16,192]{1,0:T(8,128)(2,1)S(1)}) fusion(bf16[4,16,192]{2,1,0:T(8,128)(2,1)} %token_attention.1, s32[]{:T(128)S(6)} %select_n.19, s32[]{:T(128)S(6)} %select_n.21, s32[]{:T(128)S(6)} %select_n.20), kind=kLoop, calls=%fused_computation.12 | loop fusion | bytes 36876 | tf_op jit(solution)/shard_map/jit(dynamic_index_in_dim)/squeeze | solution.py:207
  53.4 0.0 collective-permute-start.6
  53.4 1.7 %collective-permute-start.7 = (bf16[16,192]{1,0:T(8,128)(2,1)S(1)}, bf16[16,192]{1,0:T(8,128)(2,1)S(1)}, u32[]{:S(2)}, u32[]{:S(2)}) collective-permute-start(bf16[16,192]{1,0:T(8,128)(2,1)S(1)} %get-tuple-element.14), channel_id=1, source_target_pairs={{0,2},{1,3},{2,0},{3,1},{4,6},{5,7},{6,4},{7,5},{8,10},{9,11},{10,... | collective-permute-start | bytes 18440 | tf_op jit(solution)/shard_map/ppermute | solution.py:209
  55.1 0.2 collective-permute-start.8
  55.3 1.7 %pair_order.1 = bf16[16,32,128]{2,1,0:T(8,128)(2,1)} custom-call(bf16[32,24,128]{2,1,0:T(8,128)(2,1)} %copy-done), custom_call_target="tpu_custom_call" | custom-call | tf_op jit(solution)/shard_map/pair_order/pallas_call | solution.py:289
  56.9 0.0 collective-permute-done.6
  57.0 0.1 collective-permute-done.7
  57.1 1.1 %collective-permute-done.8 = bf16[16,192]{1,0:T(8,128)(2,1)S(1)} collective-permute-done((bf16[16,192]{1,0:T(8,128)(2,1)S(1)}, bf16[16,192]{1,0:T(8,128)(2,1)S(1)}, u32[]{:S(2)}, u32[]{:S(2)}) %collective-permute-start.8) | collective-permute-done | bytes 6176 | tf_op jit(solution)/shard_map/ppermute | solution.py:209
  58.2 1.3 %fusion.2 = bf16[16,192]{1,0:T(8,128)(2,1)} fusion(bf16[16,192]{1,0:T(8,128)(2,1)S(1)} %collective-permute-done.8, bf16[16,192]{1,0:T(8,128)(2,1)S(1)} %collective-permute-done.7, bf16[16,192]{1,0:T(8,128)(2,1)S(1)} %collective-permute-done.6, bf16[4,16,192]{2,1,0:T(8,128)(2,1)} %token_attention.1, s32[]{:T(128)S(6)} %select_n.18), kind=kLoop, calls=%fused_computation.9 | loop fusion | flops 24576 | bytes 30724 | tf_op jit(solution)/shard_map/convert_element_type | solution.py:285
  (2 shorter events, 0.0 us)
Async XLA Ops:
  2.1 3.1 %collective-permute-start = (bf16[128,128]{1,0:T(8,128)(2,1)S(1)}, bf16[128,128]{1,0:T(8,128)(2,1)S(1)}, u32[]{:S(2)}, u32[]{:S(2)}) collective-permute-start(bf16[128,128]{1,0:T(8,128)(2,1)S(1)} %get-tuple-element.10), channel_id=1, source_target_pairs={{0,1},{1,0},{2,3},{3,2},{4,5},{5,4},{6,7},{7,6},{8,9},{9,8},{10,11... | collective-permute-start | bytes 98312 | tf_op jit(solution)/shard_map/ppermute | solution.py:209
  2.6 4.5 %collective-permute-start.1 = (bf16[128,128]{1,0:T(8,128)(2,1)S(1)}, bf16[128,128]{1,0:T(8,128)(2,1)S(1)}, u32[]{:S(2)}, u32[]{:S(2)}) collective-permute-start(bf16[128,128]{1,0:T(8,128)(2,1)S(1)} %get-tuple-element.9), channel_id=1, source_target_pairs={{0,2},{1,3},{2,0},{3,1},{4,6},{5,7},{6,4},{7,5},{8,10},{9,11},{10,... | collective-permute-start | bytes 98312 | tf_op jit(solution)/shard_map/ppermute | solution.py:209
  5.1 3.3 %collective-permute-start.2 = (bf16[128,128]{1,0:T(8,128)(2,1)S(1)}, bf16[128,128]{1,0:T(8,128)(2,1)S(1)}, u32[]{:S(2)}, u32[]{:S(2)}) collective-permute-start(bf16[128,128]{1,0:T(8,128)(2,1)S(1)} %get-tuple-element.8), channel_id=1, source_target_pairs={{0,3},{1,2},{2,1},{3,0},{4,7},{5,6},{6,5},{7,4},{8,11},{9,10},{10,... | collective-permute-start | bytes 98312 | tf_op jit(solution)/shard_map/ppermute | solution.py:209
  5.2 3.2 %copy-start.5 = (bf16[128,128]{1,0:T(8,128)(2,1)}, bf16[128,128]{1,0:T(8,128)(2,1)S(1)}, u32[]{:S(2)}) copy-start(bf16[128,128]{1,0:T(8,128)(2,1)S(1)} %collective-permute-done.refs_1_) | copy-start | bytes 98308
  7.1 1.3 %copy-start.6 = (bf16[128,128]{1,0:T(8,128)(2,1)}, bf16[128,128]{1,0:T(8,128)(2,1)S(1)}, u32[]{:S(2)}) copy-start(bf16[128,128]{1,0:T(8,128)(2,1)S(1)} %collective-permute-done.1.refs_2_) | copy-start | bytes 98308
  8.4 0.6 %copy-start.7 = (bf16[128,128]{1,0:T(8,128)(2,1)}, bf16[128,128]{1,0:T(8,128)(2,1)S(1)}, u32[]{:S(2)}) copy-start(bf16[128,128]{1,0:T(8,128)(2,1)S(1)} %collective-permute-done.2.refs_3_) | copy-start | bytes 98308
  29.3 2.7 %copy-start.8 = (f32[768]{0:T(1024)S(1)}, f32[768]{0:T(1024)}, u32[]{:S(2)}) copy-start(f32[768]{0:T(1024)} %param.30) | copy-start | bytes 9220
  29.3 20.3 %all-to-all-start.1 = ((bf16[32,24,128]{2,1,0:T(8,128)(2,1)}), bf16[32,24,128]{2,1,0:T(8,128)(2,1)S(1)}, u32[]{:S(2)}, u32[]{:S(2)}) async-start(bf16[32,24,128]{2,1,0:T(8,128)(2,1)} %col_pass.1), calls=%async_computation.1 | async-start | bytes 393216 | tf_op jit(solution)/shard_map/all_to_all | solution.py:253
  35.0 8.8 %copy-start.1 = (bf16[2,16,192]{2,1,0:T(8,128)(2,1)S(1)}, bf16[2,16,192]{2,1,0:T(8,128)(2,1)}, u32[]{:S(2)}) copy-start(bf16[2,16,192]{2,1,0:T(8,128)(2,1)} %get-tuple-element.7) | copy-start | bytes 36868
  35.0 4.1 %collective-permute-start.3 = (bf16[1,2,16,192]{3,2,1,0:T(8,128)(2,1)}, bf16[1,2,16,192]{3,2,1,0:T(8,128)(2,1)S(1)}, u32[]{:S(2)}, u32[]{:S(2)}) collective-permute-start(bf16[1,2,16,192]{3,2,1,0:T(8,128)(2,1)} %bitcast.32), channel_id=1, source_target_pairs={{0,4},{4,0},{8,12},{12,8},{16,20},{20,16},{24,28},{28,24},{1,5},{5... | collective-permute-start | bytes 36872 | tf_op jit(solution)/shard_map/ppermute | solution.py:270
  39.1 4.7 %copy-start.2 = (bf16[1,2,16,192]{3,2,1,0:T(8,128)(2,1)}, bf16[1,2,16,192]{3,2,1,0:T(8,128)(2,1)S(1)}, u32[]{:S(2)}) copy-start(bf16[1,2,16,192]{3,2,1,0:T(8,128)(2,1)S(1)} %collective-permute-done.3.refs_1_) | copy-start | bytes 36868
  39.8 4.0 %collective-permute-start.4 = (bf16[2,2,16,192]{3,2,1,0:T(8,128)(2,1)S(1)}, bf16[2,2,16,192]{3,2,1,0:T(8,128)(2,1)S(1)}, u32[]{:S(2)}, u32[]{:S(2)}) collective-permute-start(bf16[2,2,16,192]{3,2,1,0:T(8,128)(2,1)S(1)} %pad_maximum_fusion.1), channel_id=1, source_target_pairs={{0,8},{4,12},{8,0},{12,4},{16,24},{20,28},{24,16},{28,20},{1,9},{5... | collective-permute-start | bytes 73736 | tf_op jit(solution)/shard_map/ppermute | solution.py:270
  43.8 0.6 %copy-start.3 = (bf16[2,2,16,192]{3,2,1,0:T(8,128)(2,1)}, bf16[2,2,16,192]{3,2,1,0:T(8,128)(2,1)S(1)}, u32[]{:S(2)}) copy-start(bf16[2,2,16,192]{3,2,1,0:T(8,128)(2,1)S(1)} %collective-permute-done.4.refs_2_) | copy-start | bytes 73732
  44.4 5.2 %collective-permute-start.5 = (bf16[4,2,16,192]{3,2,1,0:T(8,128)(2,1)S(1)}, bf16[4,2,16,192]{3,2,1,0:T(8,128)(2,1)S(1)}, u32[]{:S(2)}, u32[]{:S(2)}) collective-permute-start(bf16[4,2,16,192]{3,2,1,0:T(8,128)(2,1)S(1)} %pad_maximum_fusion), channel_id=1, source_target_pairs={{0,16},{4,20},{8,24},{12,28},{16,0},{20,4},{24,8},{28,12},{1,17},{... | collective-permute-start | bytes 147464 | tf_op jit(solution)/shard_map/ppermute | solution.py:270
  49.6 0.6 %copy-start.4 = (bf16[4,2,16,192]{3,2,1,0:T(8,128)(2,1)}, bf16[4,2,16,192]{3,2,1,0:T(8,128)(2,1)S(1)}, u32[]{:S(2)}) copy-start(bf16[4,2,16,192]{3,2,1,0:T(8,128)(2,1)S(1)} %collective-permute-done.5.refs_3_) | copy-start | bytes 147460
  49.6 0.7 %copy-start = (bf16[32,24,128]{2,1,0:T(8,128)(2,1)}, bf16[32,24,128]{2,1,0:T(8,128)(2,1)S(1)}, u32[]{:S(2)}) copy-start(bf16[32,24,128]{2,1,0:T(8,128)(2,1)S(1)} %all-to-all-done.1.got_ref) | copy-start | bytes 589828
  53.4 3.5 %collective-permute-start.6 = (bf16[16,192]{1,0:T(8,128)(2,1)S(1)}, bf16[16,192]{1,0:T(8,128)(2,1)S(1)}, u32[]{:S(2)}, u32[]{:S(2)}) collective-permute-start(bf16[16,192]{1,0:T(8,128)(2,1)S(1)} %get-tuple-element.12), channel_id=1, source_target_pairs={{0,1},{1,0},{2,3},{3,2},{4,5},{5,4},{6,7},{7,6},{8,9},{9,8},{10,11... | collective-permute-start | bytes 18440 | tf_op jit(solution)/shard_map/ppermute | solution.py:209
  53.4 3.7 %collective-permute-start.7 = (bf16[16,192]{1,0:T(8,128)(2,1)S(1)}, bf16[16,192]{1,0:T(8,128)(2,1)S(1)}, u32[]{:S(2)}, u32[]{:S(2)}) collective-permute-start(bf16[16,192]{1,0:T(8,128)(2,1)S(1)} %get-tuple-element.14), channel_id=1, source_target_pairs={{0,2},{1,3},{2,0},{3,1},{4,6},{5,7},{6,4},{7,5},{8,10},{9,11},{10,... | collective-permute-start | bytes 18440 | tf_op jit(solution)/shard_map/ppermute | solution.py:209
  55.1 3.1 %collective-permute-start.8 = (bf16[16,192]{1,0:T(8,128)(2,1)S(1)}, bf16[16,192]{1,0:T(8,128)(2,1)S(1)}, u32[]{:S(2)}, u32[]{:S(2)}) collective-permute-start(bf16[16,192]{1,0:T(8,128)(2,1)S(1)} %get-tuple-element.13), channel_id=1, source_target_pairs={{0,3},{1,2},{2,1},{3,0},{4,7},{5,6},{6,5},{7,4},{8,11},{9,10},{10,... | collective-permute-start | bytes 18440 | tf_op jit(solution)/shard_map/ppermute | solution.py:209

commit v2 on v1

v2 whole, which is shorter than its diff:
```python
import functools
import math

import jax
import jax.numpy as jnp
from jax import lax
from jax.experimental import pallas as pl
from jax.experimental.pallas import tpu as pltpu
from jax.sharding import PartitionSpec as P


C = 128
TRI_DIM = 16
HEAD_DIM = 48
LANES = 128

epsilon = 1e-05
cap_value = 10.0
rel_reach = 32.0

F32 = jnp.float32
BF16 = jnp.bfloat16
VMEM = pl.BlockSpec(memory_space=pltpu.VMEM)
SMEM = pl.BlockSpec(memory_space=pltpu.SMEM)
ANY = pl.BlockSpec(memory_space=pl.ANY)


def on_chip(x):
    return pltpu.with_memory_space_constraint(x, pltpu.VMEM)


def call(kernel, out_shape, smem, near=(), far=(), scratch=()):
    many = isinstance(out_shape, (tuple, list))
    return pl.pallas_call(
        kernel,
        out_shape=out_shape,
        in_specs=[SMEM] * len(smem) + [VMEM] * len(near) + [ANY] * len(far),
        out_specs=tuple([VMEM] * len(out_shape)) if many else VMEM,
        scratch_shapes=list(scratch),
    )(*smem, *[on_chip(x) for x in near], *far)


def chip(x):
    return pltpu.VMEM(x.shape, x.dtype)


def mm(a, b):
    return jnp.dot(a, b, preferred_element_type=F32)


def mm_nt(a, b):
    return lax.dot_general(a, b, (((1,), (1,)), ((), ())), preferred_element_type=F32)


def mm_tn(a, b):
    return lax.dot_general(a, b, (((0,), (0,)), ((), ())), preferred_element_type=F32)


def iota(shape, dim):
    return lax.broadcasted_iota(jnp.int32, shape, dim)


def layer_norm(x, gain):
    centered = x - jnp.mean(x, -1, keepdims=True)
    spread = jnp.mean(centered * centered, -1, keepdims=True)
    return centered * lax.rsqrt(spread + epsilon) * gain


def feature(x):
    return jnp.where(x > 0, x + 1.0, jnp.exp(jnp.minimum(x, 0.0)))


def sigmoid(x):
    return 1.0 / (1.0 + jnp.exp(-x))


def triangle(x, lines, length, gain, qk, vg, out, scale):
    tokens = x.shape[0] // lines
    normed = layer_norm(x, gain).astype(BF16)
    query_key = mm(normed, qk)
    value_gate = mm(normed, vg)
    valid = iota((tokens, C), 0) < length
    same_head = (iota((C, C), 0) // TRI_DIM) == (iota((C, C), 1) // TRI_DIM)
    lines_out = []
    for line in range(lines):
        rows = slice(line * tokens, (line + 1) * tokens)
        query = feature(query_key[rows, :C]).astype(BF16)
        key = jnp.where(valid, feature(query_key[rows, C:]), 0.0).astype(BF16)
        values = value_gate[rows, :C].astype(BF16)
        state = jnp.where(same_head, mm_tn(key, values) * scale, 0.0).astype(BF16)
        update = (sigmoid(value_gate[rows, C:]) * mm(query, state)).astype(BF16)
        lines_out.append(x[rows] + mm(update, out))
    return lines_out


def row_kernel(scale, n_col, lines, mask_ref, gain_ref, qk_ref, vg_ref, out_w_ref, own_ref, *refs):
    pieces, z_ref, x_scr, z_scr = refs[:-3], refs[-3], refs[-2], refs[-1]
    block = own_ref.shape[0] // lines
    tokens = block * n_col
    me = lax.axis_index("col")
    for k in range(n_col):
        source = me ^ k
        for line in range(lines):
            start = pl.multiple_of(line * tokens + source * block, block)
            rows = slice(line * block, (line + 1) * block)
            piece = pieces[k - 1][rows, :] if k else own_ref[rows, :]
            x_scr[pl.ds(start, block), :] = piece.astype(F32)
    length = jnp.sum(mask_ref[...])
    done = triangle(
        x_scr[...], lines, length, gain_ref[0:1, :], qk_ref[0], vg_ref[0], out_w_ref[0], scale
    )
    for line in range(lines):
        z_scr[line * tokens : (line + 1) * tokens, :] = done[line]
    owners, per_owner, _ = z_ref.shape
    for d in range(owners):
        z_ref[d] = z_scr[pl.ds(d, per_owner, stride=owners), :].astype(BF16)


def bias_form(row_count, lines, heads_here):
    side = LANES // (row_count * lines)
    return side, heads_here // side


def col_kernel(
    scale, n_row, n_col, row_count, col_count, heads_here,
    mask_ref, gain_ref, qk_ref, vg_ref, out_w_ref, bias_gain_ref, bias_proj_ref, z_ref, out_ref, z_scr, out_scr,
):
    lines = z_scr.shape[0] // (n_row * row_count)
    tokens = n_row * row_count
    devices = n_row * n_col
    z_scr[...] = z_ref[...].astype(F32)
    x = jnp.concatenate([z_scr[pl.ds(line, tokens, stride=lines), :] for line in range(lines)], axis=0)
    length = jnp.sum(mask_ref[...])
    done = triangle(x, lines, length, gain_ref[1:2, :], qk_ref[1], vg_ref[1], out_w_ref[1], scale)
    done = [part.astype(BF16).astype(F32) for part in done]
    normed = [layer_norm(part, bias_gain_ref[...]).astype(BF16) for part in done]
    side, deep = bias_form(row_count, lines, heads_here)
    chunk = row_count + deep
    proj = bias_proj_ref[...].astype(F32)
    projs = []
    for g in range(side):
        first = [c * heads_here + g * deep for c in range(n_col)]
        projs.append(jnp.concatenate([proj[f : f + deep] for f in first], axis=0).astype(BF16))
    for r in range(n_row):
        rows = slice(r * row_count, (r + 1) * row_count)
        here = jnp.concatenate([part[rows] for part in normed], axis=0)
        bias = jnp.concatenate([mm_nt(p, here) for p in projs], axis=1)
        for c in range(n_col):
            base = (r * n_col + c) * chunk
            out_scr[base : base + row_count, :] = done[c * col_count // devices][rows]
            out_scr[base + row_count : base + chunk, :] = bias[c * deep : (c + 1) * deep, :]
    out_ref[...] = out_scr[...].astype(BF16)


def start_all(pairs, sems):
    copies = [pltpu.make_async_copy(a, b, sems.at[n]) for n, (a, b) in enumerate(pairs)]
    for copy in copies:
        copy.start()
    return copies


def wait_all(copies):
    for copy in copies:
        copy.wait()


def kv_kernel(count, single_ref, gain_ref, wk_ref, wv_ref, x_ref, *refs):
    rest, (kv_ref, normed_ref, own_ref), rest_out, sems = (
        refs[:count], refs[count : count + 3], refs[count + 3 : -1], refs[-1],
    )
    copies = start_all([(x_ref.at[lax.axis_index("col")], own_ref), *zip(rest, rest_out)], sems)
    gain = gain_ref[...]
    gains = jnp.concatenate([gain[c : c + 1, :] for c in range(gain.shape[0])], axis=1)
    normed = layer_norm(single_ref[...].astype(F32), gains).astype(BF16)
    normed_ref[...] = normed
    kv_ref[0] = mm_nt(normed, wk_ref[...]).astype(BF16)
    kv_ref[1] = mm_nt(normed, wv_ref[...]).astype(BF16)
    wait_all(copies)


def qg_kernel(count, normed_ref, qk_ref, vg_ref, *refs):
    rest, (q_ref, g_ref), rest_out, (wq, wg, sems) = (
        refs[:count], refs[count : count + 2], refs[count + 2 : -3], refs[-3:],
    )
    copies = start_all([(qk_ref.at[0], wq), (vg_ref.at[1], wg), *zip(rest, rest_out)], sems)
    copies[0].wait()
    q_ref[...] = mm_nt(normed_ref[...], wq[...]).astype(BF16)
    copies[1].wait()
    g_ref[...] = mm_nt(normed_ref[...], wg[...])
    wait_all(copies[2:])


def attn_kernel(
    n_row, n_col, row_count, heads_here,
    slots, chain_bias_ref, slope_ref, mask_ref, chain_ref, residue_ref, q_ref, g_ref, out_w_ref, got_ref, *refs,
):
    kv_refs, o_refs, (k_scr, v_scr, o_scr, got_scr) = refs[: -4 - n_col], refs[-4 - n_col : -4], refs[-4:]
    tokens = n_row * row_count
    devices = n_row * n_col
    lines = tokens // devices
    width = heads_here * HEAD_DIM
    me = lax.axis_index("row")
    held = [(ref, t) for ref in kv_refs for t in range(ref.shape[0])]
    for slot, (ref, t) in zip(slots, held):
        start = pl.multiple_of((me ^ slot) * row_count, row_count)
        k_scr[pl.ds(start, row_count), :] = ref[t, 0].astype(F32)
        v_scr[pl.ds(start, row_count), :] = ref[t, 1].astype(F32)
    keys, values = k_scr[...].astype(BF16), v_scr[...].astype(BF16)

    own = iota((row_count, tokens), 1) == iota((row_count, tokens), 0) + me * row_count
    chain = chain_ref[...].astype(F32)
    residue = residue_ref[...].astype(F32)
    my_chain = jnp.sum(jnp.where(own, chain, 0.0), -1, keepdims=True)
    my_residue = jnp.sum(jnp.where(own, residue, 0.0), -1, keepdims=True)
    same_chain = my_chain == chain
    offset = jnp.clip(my_residue - residue, -rel_reach, rel_reach) / rel_reach
    length = jnp.sum(mask_ref[...])
    valid = iota((row_count, tokens), 1) < length

    _, deep = bias_form(row_count, lines, heads_here)
    chunk = row_count + deep
    got_scr[...] = got_ref[...].astype(F32)
    same = (iota((devices, devices), 0) == iota((devices, devices), 1)).astype(F32).astype(BF16)
    turned = [
        mm_tn(got_scr[pl.ds(row_count + a, devices, stride=chunk), :].astype(BF16), same) for a in range(deep)
    ]

    head_of = iota((row_count, width), 1) // HEAD_DIM
    query = q_ref[...].astype(F32)
    stacked = jnp.concatenate(
        [jnp.where(head_of == h, query, 0.0) for h in range(heads_here)], axis=0
    ).astype(BF16)
    scores = mm_nt(stacked, keys) / math.sqrt(HEAD_DIM)
    weights = []
    for h in range(heads_here):
        bias = jnp.concatenate(
            [
                turned[h % deep][(h // deep * lines + line) * row_count :][:row_count]
                for line in range(lines)
            ],
            axis=1,
        )
        e = scores[h * row_count : (h + 1) * row_count] + bias
        e = e + jnp.where(same_chain, chain_bias_ref[0:1, h : h + 1] + slope_ref[0:1, h : h + 1] * offset, 0.0)
        weights.append(jnp.where(valid, jnp.exp(cap_value * jnp.tanh(e / cap_value)), 0.0))
    numerator = mm(jnp.concatenate(weights, axis=0).astype(BF16), values)
    attended = jnp.zeros((row_count, width), F32)
    for h in range(heads_here):
        part = numerator[h * row_count : (h + 1) * row_count] / jnp.sum(weights[h], -1, keepdims=True)
        attended = jnp.where(head_of == h, part, attended)
    gated = (sigmoid(g_ref[...]) * attended).astype(BF16)
    full = mm(gated, out_w_ref[...])
    share = full.shape[1] // n_col
    for c in range(n_col):
        o_scr[c] = full[:, c * share : (c + 1) * share]
    for k in range(n_col):
        o_refs[k][...] = o_scr[lax.axis_index("col") ^ k].astype(BF16)


def pair_kernel(row_count, chunk, got_ref, out_ref, scr):
    scr[...] = got_ref[...].astype(F32)
    for i in range(row_count):
        out_ref[i] = scr[pl.ds(i, out_ref.shape[1], stride=chunk), :].astype(BF16)


def pick_kernel(n_col, x_ref, single_ref, gain_ref, qk_ref, vg_ref, *refs):
    sent, (single_out, gain_out, wk_out, wv_out, sems) = refs[: n_col - 1], refs[n_col - 1 :]
    me = lax.axis_index("col")
    pairs = [(x_ref.at[me ^ (k + 1)], sent[k]) for k in range(n_col - 1)]
    pairs += [(qk_ref.at[1], wk_out), (vg_ref.at[0], wv_out), (single_ref, single_out), (gain_ref, gain_out)]
    wait_all(start_all(pairs, sems))


def swap_col(blocks, n_col):
    got = []
    for k, block in enumerate(blocks, 1):
        got.append(lax.ppermute(block, "col", [(i, i ^ k) for i in range(n_col)]))
    return got


def in_layer(n_row, n_col, *args):
    return on_device(n_row, n_col, *args)


def on_device(
    n_row, n_col,
    pair_act, single, token_mask, chain_index, residue_index, tri_gain, tri_qk, tri_vg, tri_out,
    bias_gain, bias_proj, chain_bias, pos_slope, attn_gain, attn_qk, attn_vg, attn_out,
):
    tokens = token_mask.shape[0]
    row_count, col_count = pair_act.shape[0], pair_act.shape[1]
    heads_here = chain_bias.shape[0]
    devices = n_row * n_col
    own_rows, own_cols = row_count // n_col, tokens // devices
    scale = 1.0 / (2.0 * TRI_DIM * math.sqrt(tokens))
    width = heads_here * HEAD_DIM
    share = attn_out.shape[1] // n_col
    chunk = row_count + bias_form(row_count, own_cols, heads_here)[1]

    blocks = pair_act.reshape(n_col, own_rows * col_count, C)
    block = pltpu.VMEM(blocks.shape[1:], BF16)
    gain2 = attn_gain.reshape(-1, C)
    wqk, wvg = attn_qk.swapaxes(1, 2), attn_vg.swapaxes(1, 2)
    weight = pltpu.VMEM(wqk.shape[1:], BF16)
    *picked, single, gain2, wk, wv = call(
        functools.partial(pick_kernel, n_col),
        [block] * (n_col - 1) + [chip(single), chip(gain2), weight, weight],
        [], [], [blocks, single, gain2, wqk, wvg], [pltpu.SemaphoreType.DMA((n_col + 3,))],
    )
    pieces = swap_col(picked, n_col)
    early = [token_mask.reshape(1, tokens), tri_gain, tri_qk, tri_vg, tri_out]
    kv, normed, own, *early = call(
        functools.partial(kv_kernel, len(early)),
        [pltpu.VMEM((2, row_count, width), BF16), chip(single), block, *map(chip, early)],
        [], [single, gain2, wk, wv], [blocks, *early], [pltpu.SemaphoreType.DMA((1 + len(early),))],
    )
    mask, tri_gain, tri_qk, tri_vg, tri_out = early
    z_out = call(
        functools.partial(row_kernel, scale, n_col, own_rows),
        pltpu.VMEM((devices, own_rows * own_cols, C), BF16),
        [], [mask, tri_gain, tri_qk, tri_vg, tri_out, own, *pieces],
        scratch=[pltpu.VMEM((own_rows * tokens, C), F32)] * 2,
    )

    z_in = lax.all_to_all(z_out, ("row", "col"), 0, 0, tiled=True)
    late = [
        bias_gain.reshape(1, C), bias_proj.T, chain_bias.reshape(1, -1), pos_slope.reshape(1, -1),
        chain_index.reshape(1, tokens), residue_index.reshape(1, tokens), attn_out,
    ]
    query, gate, *late = call(
        functools.partial(qg_kernel, len(late)),
        [pltpu.VMEM((row_count, width), BF16), pltpu.VMEM((row_count, width), F32), *map(chip, late)],
        [], [normed], [wqk, wvg, *late], [weight, weight, pltpu.SemaphoreType.DMA((2 + len(late),))],
    )
    bias_gain, bias_proj, chain_bias, pos_slope, chain, residue, attn_out = late
    back = call(
        functools.partial(col_kernel, scale, n_row, n_col, row_count, col_count, heads_here),
        pltpu.VMEM((devices * chunk, C), BF16),
        [],
        [
            mask, tri_gain, tri_qk, tri_vg, tri_out, bias_gain, bias_proj,
            z_in.reshape(own_cols * tokens, C),
        ],
        scratch=[pltpu.VMEM((own_cols * tokens, C), F32), pltpu.VMEM((devices * chunk, C), F32)],
    )
    got = lax.all_to_all(back.reshape(devices, chunk // 2, 2, C), ("row", "col"), 0, 0, tiled=True)
    got = got.reshape(devices * chunk, C)

    held, slots = [kv[None]], [0]
    for step in kv_steps(n_row):
        sent = held[0] if len(held) == 1 else jnp.concatenate(held, axis=0)
        held.append(lax.ppermute(sent, "row", [(i, i ^ step) for i in range(n_row)]))
        slots += [slot ^ step for slot in slots]

    terms = call(
        functools.partial(attn_kernel, n_row, n_col, row_count, heads_here, slots),
        [pltpu.VMEM((row_count, share), BF16)] * n_col,
        [],
        [chain_bias, pos_slope, mask, chain, residue, query, gate, attn_out, got, *held],
        scratch=[pltpu.VMEM((tokens, width), F32)] * 2
        + [pltpu.VMEM((n_col, row_count, share), F32), pltpu.VMEM((devices * chunk, C), F32)],
    )
    parts = [terms[0]] + swap_col(terms[1:], n_col)
    token_update = sum(part.astype(F32) for part in parts).astype(BF16)

    first = lax.axis_index("col") * col_count % devices
    mine = got if col_count == devices else lax.dynamic_slice_in_dim(got, first * chunk, col_count * chunk, 0)
    pair_out = call(
        functools.partial(pair_kernel, row_count, chunk),
        jax.ShapeDtypeStruct((row_count, col_count, C), BF16),
        [], [mine], scratch=[pltpu.VMEM((col_count * chunk, C), F32)],
    )
    return (pair_out, token_update)


def kv_steps(n_row):
    return [1 << b for b in range((n_row - 1).bit_length())]


def solution(mesh):
    return jax.shard_map(
        functools.partial(in_layer, mesh.shape["row"], mesh.shape["col"]),
        mesh=mesh,
        in_specs=(
            P(("grp", "row"), "col", None),
            P(("grp", "row"), None),
            P("grp"),
            P("grp"),
            P("grp"),
            P(),
            P(),
            P(),
            P(),
            P(),
            P(),
            P("col"),
            P("col"),
            P(),
            P(None, None, "col"),
            P(None, None, "col"),
            P("col", None),
        ),
        out_specs=(P(("grp", "row"), "col", None), P(("grp", "row"), "col")),
        check_vma=False,
    )
```

time: 60.1 us -> 46.9 us (0.78)
  blocking collectives: 13.6 us -> 0 us
  starting transfers between devices: 13.6 us -> 20.2 us
  local copies, waits for them, and re-layouts: 4.65 us -> 0 us
  waiting for transfers between devices: 11.7 us -> 14.9 us
  Pallas kernels: 13.2 us -> 10.1 us
  other arithmetic: 2.05 us -> 0.63 us
    all_to_all x1 -> x0, blocking collectives: 13.6 us -> none  [on_device(): z_in = lax.all_to_all(z_out, ('row', 'col'), 0, 0, tiled=True)]
    all_to_all x1 -> x2, starting transfers between devices: 2.71 us -> 7.81 us  [the longest x1 5.23 us: on_device(): z_in = lax.all_to_all(z_out, ('row', 'col'), 0, 0, tiled=True)]
    all_to_all x1 -> x2, waiting for transfers between devices: 0.01 us -> 4.77 us  [the longest x1 4.77 us: on_device(): z_in = lax.all_to_all(z_out, ('row', 'col'), 0, 0, tiled=True)]
    pallas_call x5 -> x7, Pallas kernels: 13.2 us -> 10.1 us  [call(): pl.pallas_call(kernel, out_shape=out_shape, in_specs=[SMEM] * len(smem) +...]
    squeeze x2 -> x0, local copies, waits for them, and re-layouts: 2.16 us -> none  [swap_col(): piece = lax.dynamic_index_in_dim(blocks, me ^ k, 0, keepdims=False)]
    unnamed x18 -> x0, local copies, waits for them, and re-layouts: 1.9 us -> none
    ppermute x3, starting transfers between devices: 5.94 us -> 7.33 us  [on_device(): lax.ppermute(sent, 'row', [(i, i ^ step) for i in range(n_row)])]
    ppermute x3, waiting for transfers between devices: 7.27 us -> 6.07 us  [on_device(): lax.ppermute(sent, 'row', [(i, i ^ step) for i in range(n_row)])]
  transfers between devices with their start and end apart: 10 -> 11, of which waited for: 7 -> 7; matrix products, arithmetic and copies ran while one was open for 2% -> 0% of each run, Pallas kernels for 7% -> 13%
where the time goes in v2:
time: 46.9 us; the launch traced here: 46.6 us
  starting transfers between devices  20.2 us (43%)
  waiting for transfers between devices  14.9 us (32%)
  Pallas kernels  10.1 us (22%)
  between operations  0.72 us (2%)
  other arithmetic  0.63 us (1%)
    pallas_call x7, Pallas kernels, call(): pl.pallas_call(kernel, out_shape=out_shape, in_specs=[SMEM] * len(smem) +...  10.1 us
    ppermute x3, starting transfers between devices, on_device(): lax.ppermute(sent, 'row', [(i, i ^ step) for i in range(n_row)])  7.33 us
    ppermute x3, waiting for transfers between devices, on_device(): lax.ppermute(sent, 'row', [(i, i ^ step) for i in range(n_row)])  6.07 us
    all_to_all x1, starting transfers between devices, on_device(): z_in = lax.all_to_all(z_out, ('row', 'col'), 0, 0, tiled=True)  5.23 us
    ppermute x6, starting transfers between devices, swap_col(): got.append(lax.ppermute(block, 'col', [(i, i ^ k) for i in range(n_col)]))  5.07 us
    all_to_all x1, waiting for transfers between devices, on_device(): z_in = lax.all_to_all(z_out, ('row', 'col'), 0, 0, tiled=True)  4.77 us
    ppermute x6, waiting for transfers between devices, swap_col(): got.append(lax.ppermute(block, 'col', [(i, i ^ k) for i in range(n_col)]))  4.08 us
    all_to_all x1, starting transfers between devices, on_device(): lax.all_to_all(back.reshape(devices, chunk // 2, 2, C), ('row', 'col'), 0...  2.57 us
  transfers between devices with their start and end apart: 11, of which 7 were waited for; matrix products, arithmetic and copies ran while one was open for 0% of the time, Pallas kernels for 13%

profile of v2, /device:TPU:0, one launch (start us, length us, event | category | flops | bytes accessed | tf_op | source)
XLA Modules:
  0.0 46.6 jit_solution(15846524911460332661)
XLA Ops:
  0.6 1.2 %shard_map.176 = (bf16[128,128]{1,0:T(8,128)(2,1)S(1)}, bf16[128,128]{1,0:T(8,128)(2,1)S(1)}, bf16[128,128]{1,0:T(8,128)(2,1)S(1)}, bf16[16,768]{1,0:T(8,128)(2,...) custom-call(bf16[4,128,128]{2,1,0:T(8,128)(2,1)} %bitcast.26, ...), custom_call_target="tpu_custom_call" | custom-call | tf_op jit(solution)/shard_map/pallas_call | solution.py:34
  1.8 0.6 %collective-permute-start = (bf16[128,128]{1,0:T(8,128)(2,1)S(1)}, bf16[128,128]{1,0:T(8,128)(2,1)S(1)}, u32[]{:S(2)}, u32[]{:S(2)}) collective-permute-start(bf16[128,128]{1,0:T(8,128)(2,1)S(1)} %get-tuple-element.43), channel_id=1, source_target_pairs={{0,1},{1,0},{2,3},{3,2},{4,5},{5,4},{6,7},{7,6},{8,9},{9,8},{10,11... | collective-permute-start | bytes 98312 | tf_op jit(solution)/shard_map/ppermute | solution.py:277
  2.4 2.6 %collective-permute-start.1 = (bf16[128,128]{1,0:T(8,128)(2,1)S(1)}, bf16[128,128]{1,0:T(8,128)(2,1)S(1)}, u32[]{:S(2)}, u32[]{:S(2)}) collective-permute-start(bf16[128,128]{1,0:T(8,128)(2,1)S(1)} %get-tuple-element.44), channel_id=1, source_target_pairs={{0,2},{1,3},{2,0},{3,1},{4,6},{5,7},{6,4},{7,5},{8,10},{9,11},{10,... | collective-permute-start | bytes 98312 | tf_op jit(solution)/shard_map/ppermute | solution.py:277
  4.9 0.0 collective-permute-start.2
  5.0 1.3 %shard_map.177 = (bf16[2,16,192]{2,1,0:T(8,128)(2,1)S(1)}, bf16[16,768]{1,0:T(8,128)(2,1)S(1)}, bf16[128,128]{1,0:T(8,128)(2,1)S(1)}, s32[1,128]{1,0:T(1,128)S(1...) custom-call(bf16[16,768]{1,0:T(8,128)(2,1)S(1)} %get-tuple-element.3, ...), custom_call_target="tpu_custom_call" | custom-call | tf_op jit(solution)/shard_map/pallas_call | solution.py:34
  6.3 0.0 collective-permute-done.refs_0_
  6.3 0.6 %collective-permute-done.1.refs_1_ = bf16[128,128]{1,0:T(8,128)(2,1)S(1)} collective-permute-done((bf16[128,128]{1,0:T(8,128)(2,1)S(1)}, bf16[128,128]{1,0:T(8,128)(2,1)S(1)}, u32[]{:S(2)}, u32[]{:S(2)}) %collective-permute-start.1) | collective-permute-done | bytes 32800 | tf_op jit(solution)/shard_map/ppermute | solution.py:277
  6.9 1.4 %collective-permute-done.2.refs_2_ = bf16[128,128]{1,0:T(8,128)(2,1)S(1)} collective-permute-done((bf16[128,128]{1,0:T(8,128)(2,1)S(1)}, bf16[128,128]{1,0:T(8,128)(2,1)S(1)}, u32[]{:S(2)}, u32[]{:S(2)}) %collective-permute-start.2) | collective-permute-done | bytes 32800 | tf_op jit(solution)/shard_map/ppermute | solution.py:277
  8.3 2.1 %shard_map.179 = bf16[32,16,128]{2,1,0:T(8,128)(2,1)} custom-call(s32[1,128]{1,0:T(1,128)S(1)} %get-tuple-element.34.mask_ref, f32[2,128]{1,0:T(2,128)S(1)} %get-tuple-element.35.gain_ref, bf16[2,128,256]{2,1,0:T(8,128)(2,1)S(1)} %get-tuple-element.36.qk_ref, bf16[2,128,256]{2,1,0:T(8,128)(2,1)S(1)} %get-tuple-element.37.vg_ref, ...), custom_call_target="tpu_custom_call" | custom-call | tf_op jit(solution)/shard_map/pallas_call | solution.py:34
  10.4 5.2 %all-to-all-start = ((bf16[32,16,128]{2,1,0:T(8,128)(2,1)}), bf16[32,16,128]{2,1,0:T(8,128)(2,1)S(1)}, u32[]{:S(2)}, u32[]{:S(2)}) async-start(bf16[32,16,128]{2,1,0:T(8,128)(2,1)} %shard_map.179), calls=%async_computation | async-start | bytes 262144 | tf_op jit(solution)/shard_map/all_to_all | solution.py:325
  15.7 1.8 %collective-permute-start.3 = (bf16[1,2,16,192]{3,2,1,0:T(8,128)(2,1)S(1)}, bf16[1,2,16,192]{3,2,1,0:T(8,128)(2,1)S(1)}, u32[]{:S(2)}, u32[]{:S(2)}) collective-permute-start(bf16[1,2,16,192]{3,2,1,0:T(8,128)(2,1)S(1)} %bitcast.18), channel_id=1, source_target_pairs={{0,4},{4,0},{8,12},{12,8},{16,20},{20,16},{24,28},{28,24},{1,5},{5... | collective-permute-start | bytes 36872 | tf_op jit(solution)/shard_map/ppermute | solution.py:352
  17.5 1.6 %shard_map.178 = (bf16[16,192]{1,0:T(8,128)(2,1)S(1)}, f32[16,192]{1,0:T(8,128)S(1)}, f32[1,128]{1,0:T(1,128)S(1)}, bf16[16,128]{1,0:T(8,128)(2,1)S(1)}, f32[1,4...) custom-call(bf16[16,768]{1,0:T(8,128)(2,1)S(1)} %get-tuple-element.3, ...), custom_call_target="tpu_custom_call" | custom-call | tf_op jit(solution)/shard_map/pallas_call | solution.py:34
  19.1 4.8 %all-to-all-done = bf16[32,16,128]{2,1,0:T(8,128)(2,1)S(1)} async-done(((bf16[32,16,128]{2,1,0:T(8,128)(2,1)}), bf16[32,16,128]{2,1,0:T(8,128)(2,1)S(1)}, u32[]{:S(2)}, u32[]{:S(2)}) %all-to-all-start) | async-done | bytes 131104 | tf_op jit(solution)/shard_map/all_to_all | solution.py:325
  23.9 2.6 %shard_map.180 = bf16[576,128]{1,0:T(8,128)(2,1)} custom-call(s32[1,128]{1,0:T(1,128)S(1)} %get-tuple-element.34.mask_ref, f32[2,128]{1,0:T(2,128)S(1)} %get-tuple-element.35.gain_ref, bf16[2,128,256]{2,1,0:T(8,128)(2,1)S(1)} %get-tuple-element.36.qk_ref, bf16[2,128,256]{2,1,0:T(8,128)(2,1)S(1)} %get-tuple-element.37.vg_ref, ...), custom_call_target="tpu_custom_call" | custom-call | tf_op jit(solution)/shard_map/pallas_call | solution.py:34
  26.4 2.6 %all-to-all-start.1 = ((bf16[32,9,2,128]{3,2,1,0:T(2,128)(2,1)}), bf16[32,9,2,128]{3,2,1,0:T(2,128)(2,1)S(1)}, u32[]{:S(2)}, u32[]{:S(2)}) async-start(bf16[32,9,2,128]{3,2,1,0:T(2,128)(2,1)} %bitcast.12), calls=%async_computation.1 | async-start | bytes 294912 | tf_op jit(solution)/shard_map/all_to_all | solution.py:346
  29.0 0.0 collective-permute-done.3.refs_1_
  29.1 1.8 %collective-permute-start.4 = (bf16[2,2,16,192]{3,2,1,0:T(8,128)(2,1)S(1)}, bf16[2,2,16,192]{3,2,1,0:T(8,128)(2,1)S(1)}, u32[]{:S(2)}, u32[]{:S(2)}) collective-permute-start(bf16[2,2,16,192]{3,2,1,0:T(8,128)(2,1)S(1)} %pad_maximum_fusion.1), channel_id=1, source_target_pairs={{0,8},{4,12},{8,0},{12,4},{16,24},{20,28},{24,16},{28,20},{1,9},{5... | collective-permute-start | bytes 73736 | tf_op jit(solution)/shard_map/ppermute | solution.py:352
  30.8 2.9 %collective-permute-done.4.refs_2_ = bf16[2,2,16,192]{3,2,1,0:T(8,128)(2,1)S(1)} collective-permute-done((bf16[2,2,16,192]{3,2,1,0:T(8,128)(2,1)S(1)}, bf16[2,2,16,192]{3,2,1,0:T(8,128)(2,1)S(1)}, u32[]{:S(2)}, u32[]{:S(2)}) %collective-permute-start.4) | collective-permute-done | bytes 24608 | tf_op jit(solution)/shard_map/ppermute | solution.py:352
  33.7 3.7 %collective-permute-start.5 = (bf16[4,2,16,192]{3,2,1,0:T(8,128)(2,1)S(1)}, bf16[4,2,16,192]{3,2,1,0:T(8,128)(2,1)S(1)}, u32[]{:S(2)}, u32[]{:S(2)}) collective-permute-start(bf16[4,2,16,192]{3,2,1,0:T(8,128)(2,1)S(1)} %pad_maximum_fusion), channel_id=1, source_target_pairs={{0,16},{4,20},{8,24},{12,28},{16,0},{20,4},{24,8},{28,12},{1,17},{... | collective-permute-start | bytes 147464 | tf_op jit(solution)/shard_map/ppermute | solution.py:352
  37.4 3.2 %collective-permute-done.5.refs_3_ = bf16[4,2,16,192]{3,2,1,0:T(8,128)(2,1)S(1)} collective-permute-done((bf16[4,2,16,192]{3,2,1,0:T(8,128)(2,1)S(1)}, bf16[4,2,16,192]{3,2,1,0:T(8,128)(2,1)S(1)}, u32[]{:S(2)}, u32[]{:S(2)}) %collective-permute-start.5) | collective-permute-done | bytes 49184 | tf_op jit(solution)/shard_map/ppermute | solution.py:352
  40.6 0.0 all-to-all-done.1
  40.6 0.6 %shard_map.182 = (bf16[16,192]{1,0:T(8,128)(2,1)S(1)}, bf16[16,192]{1,0:T(8,128)(2,1)S(1)}, bf16[16,192]{1,0:T(8,128)(2,1)S(1)}, bf16[16,192]{1,0:T(8,128)(2,1)S(1)}) custom-call(f32[1,4]{1,0:T(1,128)S(1)} %get-tuple-element.46.chain_bias_ref, f32[1,4]{1,0:T(1,128)S(1)} %get-tuple-element.47.slope_ref, s32[1,128]{1,0:T(1,128)S(1)} %get-tuple-element.34.mask_ref, ...), custom_call_target="tpu_custom_call" | custom-call | tf_op jit(solution)/shard_map/pallas_call | solution.py:34
  41.3 0.1 collective-permute-start.6
  41.4 1.5 %collective-permute-start.7 = (bf16[16,192]{1,0:T(8,128)(2,1)S(1)}, bf16[16,192]{1,0:T(8,128)(2,1)S(1)}, u32[]{:S(2)}, u32[]{:S(2)}) collective-permute-start(bf16[16,192]{1,0:T(8,128)(2,1)S(1)} %get-tuple-element.56), channel_id=1, source_target_pairs={{0,2},{1,3},{2,0},{3,1},{4,6},{5,7},{6,4},{7,5},{8,10},{9,11},{10,... | collective-permute-start | bytes 18440 | tf_op jit(solution)/shard_map/ppermute | solution.py:277
  42.9 0.3 collective-permute-start.8
  43.2 0.7 %shard_map.181 = bf16[16,32,128]{2,1,0:T(8,128)(2,1)} custom-call(bf16[576,128]{1,0:T(8,128)(2,1)S(1)} %bitcast.16), custom_call_target="tpu_custom_call" | custom-call | tf_op jit(solution)/shard_map/pallas_call | solution.py:34
  43.9 0.0 collective-permute-done.6
  43.9 1.2 %collective-permute-done.7 = bf16[16,192]{1,0:T(8,128)(2,1)S(1)} collective-permute-done((bf16[16,192]{1,0:T(8,128)(2,1)S(1)}, bf16[16,192]{1,0:T(8,128)(2,1)S(1)}, u32[]{:S(2)}, u32[]{:S(2)}) %collective-permute-start.7) | collective-permute-done | bytes 6176 | tf_op jit(solution)/shard_map/ppermute | solution.py:277
  45.1 0.9 %collective-permute-done.8 = bf16[16,192]{1,0:T(8,128)(2,1)S(1)} collective-permute-done((bf16[16,192]{1,0:T(8,128)(2,1)S(1)}, bf16[16,192]{1,0:T(8,128)(2,1)S(1)}, u32[]{:S(2)}, u32[]{:S(2)}) %collective-permute-start.8) | collective-permute-done | bytes 6176 | tf_op jit(solution)/shard_map/ppermute | solution.py:277
  46.0 0.6 %add_convert_fusion = bf16[16,192]{1,0:T(8,128)(2,1)} fusion(bf16[16,192]{1,0:T(8,128)(2,1)S(1)} %collective-permute-done.8, bf16[16,192]{1,0:T(8,128)(2,1)S(1)} %collective-permute-done.7, bf16[16,192]{1,0:T(8,128)(2,1)S(1)} %collective-permute-done.6, bf16[16,192]{1,0:T(8,128)(2,1)S(1)} %get-tuple-element.54), kind=kLoop, calls=%fused_computation.2 | loop fusion | flops 24576 | bytes 30720 | tf_op jit(solution)/shard_map/convert_element_type | solution.py:364
  (2 shorter events, 0.0 us)
Async XLA Ops:
  1.8 4.5 %collective-permute-start = (bf16[128,128]{1,0:T(8,128)(2,1)S(1)}, bf16[128,128]{1,0:T(8,128)(2,1)S(1)}, u32[]{:S(2)}, u32[]{:S(2)}) collective-permute-start(bf16[128,128]{1,0:T(8,128)(2,1)S(1)} %get-tuple-element.43), channel_id=1, source_target_pairs={{0,1},{1,0},{2,3},{3,2},{4,5},{5,4},{6,7},{7,6},{8,9},{9,8},{10,11... | collective-permute-start | bytes 98312 | tf_op jit(solution)/shard_map/ppermute | solution.py:277
  2.4 4.5 %collective-permute-start.1 = (bf16[128,128]{1,0:T(8,128)(2,1)S(1)}, bf16[128,128]{1,0:T(8,128)(2,1)S(1)}, u32[]{:S(2)}, u32[]{:S(2)}) collective-permute-start(bf16[128,128]{1,0:T(8,128)(2,1)S(1)} %get-tuple-element.44), channel_id=1, source_target_pairs={{0,2},{1,3},{2,0},{3,1},{4,6},{5,7},{6,4},{7,5},{8,10},{9,11},{10,... | collective-permute-start | bytes 98312 | tf_op jit(solution)/shard_map/ppermute | solution.py:277
  4.9 3.4 %collective-permute-start.2 = (bf16[128,128]{1,0:T(8,128)(2,1)S(1)}, bf16[128,128]{1,0:T(8,128)(2,1)S(1)}, u32[]{:S(2)}, u32[]{:S(2)}) collective-permute-start(bf16[128,128]{1,0:T(8,128)(2,1)S(1)} %get-tuple-element.45), channel_id=1, source_target_pairs={{0,3},{1,2},{2,1},{3,0},{4,7},{5,6},{6,5},{7,4},{8,11},{9,10},{10,... | collective-permute-start | bytes 98312 | tf_op jit(solution)/shard_map/ppermute | solution.py:277
  10.4 13.4 %all-to-all-start = ((bf16[32,16,128]{2,1,0:T(8,128)(2,1)}), bf16[32,16,128]{2,1,0:T(8,128)(2,1)S(1)}, u32[]{:S(2)}, u32[]{:S(2)}) async-start(bf16[32,16,128]{2,1,0:T(8,128)(2,1)} %shard_map.179), calls=%async_computation | async-start | bytes 262144 | tf_op jit(solution)/shard_map/all_to_all | solution.py:325
  15.7 13.4 %collective-permute-start.3 = (bf16[1,2,16,192]{3,2,1,0:T(8,128)(2,1)S(1)}, bf16[1,2,16,192]{3,2,1,0:T(8,128)(2,1)S(1)}, u32[]{:S(2)}, u32[]{:S(2)}) collective-permute-start(bf16[1,2,16,192]{3,2,1,0:T(8,128)(2,1)S(1)} %bitcast.18), channel_id=1, source_target_pairs={{0,4},{4,0},{8,12},{12,8},{16,20},{20,16},{24,28},{28,24},{1,5},{5... | collective-permute-start | bytes 36872 | tf_op jit(solution)/shard_map/ppermute | solution.py:352
  26.4 14.2 %all-to-all-start.1 = ((bf16[32,9,2,128]{3,2,1,0:T(2,128)(2,1)}), bf16[32,9,2,128]{3,2,1,0:T(2,128)(2,1)S(1)}, u32[]{:S(2)}, u32[]{:S(2)}) async-start(bf16[32,9,2,128]{3,2,1,0:T(2,128)(2,1)} %bitcast.12), calls=%async_computation.1 | async-start | bytes 294912 | tf_op jit(solution)/shard_map/all_to_all | solution.py:346
  29.1 4.6 %collective-permute-start.4 = (bf16[2,2,16,192]{3,2,1,0:T(8,128)(2,1)S(1)}, bf16[2,2,16,192]{3,2,1,0:T(8,128)(2,1)S(1)}, u32[]{:S(2)}, u32[]{:S(2)}) collective-permute-start(bf16[2,2,16,192]{3,2,1,0:T(8,128)(2,1)S(1)} %pad_maximum_fusion.1), channel_id=1, source_target_pairs={{0,8},{4,12},{8,0},{12,4},{16,24},{20,28},{24,16},{28,20},{1,9},{5... | collective-permute-start | bytes 73736 | tf_op jit(solution)/shard_map/ppermute | solution.py:352
  33.7 7.0 %collective-permute-start.5 = (bf16[4,2,16,192]{3,2,1,0:T(8,128)(2,1)S(1)}, bf16[4,2,16,192]{3,2,1,0:T(8,128)(2,1)S(1)}, u32[]{:S(2)}, u32[]{:S(2)}) collective-permute-start(bf16[4,2,16,192]{3,2,1,0:T(8,128)(2,1)S(1)} %pad_maximum_fusion), channel_id=1, source_target_pairs={{0,16},{4,20},{8,24},{12,28},{16,0},{20,4},{24,8},{28,12},{1,17},{... | collective-permute-start | bytes 147464 | tf_op jit(solution)/shard_map/ppermute | solution.py:352
  41.3 2.6 %collective-permute-start.6 = (bf16[16,192]{1,0:T(8,128)(2,1)S(1)}, bf16[16,192]{1,0:T(8,128)(2,1)S(1)}, u32[]{:S(2)}, u32[]{:S(2)}) collective-permute-start(bf16[16,192]{1,0:T(8,128)(2,1)S(1)} %get-tuple-element.55), channel_id=1, source_target_pairs={{0,1},{1,0},{2,3},{3,2},{4,5},{5,4},{6,7},{7,6},{8,9},{9,8},{10,11... | collective-permute-start | bytes 18440 | tf_op jit(solution)/shard_map/ppermute | solution.py:277
  41.4 3.7 %collective-permute-start.7 = (bf16[16,192]{1,0:T(8,128)(2,1)S(1)}, bf16[16,192]{1,0:T(8,128)(2,1)S(1)}, u32[]{:S(2)}, u32[]{:S(2)}) collective-permute-start(bf16[16,192]{1,0:T(8,128)(2,1)S(1)} %get-tuple-element.56), channel_id=1, source_target_pairs={{0,2},{1,3},{2,0},{3,1},{4,6},{5,7},{6,4},{7,5},{8,10},{9,11},{10,... | collective-permute-start | bytes 18440 | tf_op jit(solution)/shard_map/ppermute | solution.py:277
  42.9 3.1 %collective-permute-start.8 = (bf16[16,192]{1,0:T(8,128)(2,1)S(1)}, bf16[16,192]{1,0:T(8,128)(2,1)S(1)}, u32[]{:S(2)}, u32[]{:S(2)}) collective-permute-start(bf16[16,192]{1,0:T(8,128)(2,1)S(1)} %get-tuple-element.57), channel_id=1, source_target_pairs={{0,3},{1,2},{2,1},{3,0},{4,7},{5,6},{6,5},{7,4},{8,11},{9,10},{10,... | collective-permute-start | bytes 18440 | tf_op jit(solution)/shard_map/ppermute | solution.py:277

commit v3 on v2

--- a/solution.py
+++ b/solution.py
@@ -67,30 +67,38 @@
 
 
 def feature(x):
-    return jnp.where(x > 0, x + 1.0, jnp.exp(jnp.minimum(x, 0.0)))
+    return jnp.where(x > 0, x + 1.0, jnp.exp(x))
 
 
 def sigmoid(x):
-    return 1.0 / (1.0 + jnp.exp(-x))
-
-
-def triangle(x, lines, length, gain, qk, vg, out, scale):
-    tokens = x.shape[0] // lines
+    return 0.5 * jnp.tanh(0.5 * x) + 0.5
+
+
+GROUP = 4
+
+
+def triangle_lines(lines, valid, same_head, gain, qk, vg, out, scale):
+    tokens = lines[0].shape[0]
+    x = jnp.concatenate(lines, axis=0)
     normed = layer_norm(x, gain).astype(BF16)
-    query_key = mm(normed, qk)
-    value_gate = mm(normed, vg)
-    valid = iota((tokens, C), 0) < length
+    query_key, value_gate = mm(normed, qk), mm(normed, vg)
+    each = [slice(n * tokens, (n + 1) * tokens) for n in range(len(lines))]
+    keys = [jnp.where(valid, feature(query_key[rows, C:]), 0.0).astype(BF16) for rows in each]
+    values = value_gate[:, :C].astype(BF16)
+    states = [
+        jnp.where(same_head, mm_tn(key, values[rows]) * scale, 0.0).astype(BF16) for key, rows in zip(keys, each)
+    ]
+    queries = feature(query_key[:, :C]).astype(BF16)
+    gate = sigmoid(value_gate[:, C:])
+    mixed = jnp.concatenate([mm(queries[rows], state) for state, rows in zip(states, each)], axis=0)
+    x = x + mm((gate * mixed).astype(BF16), out)
+    return [x[rows] for rows in each]
+
+
+def masks(tokens, mask_ref):
+    valid = iota((tokens, C), 0) < jnp.sum(mask_ref[...])
     same_head = (iota((C, C), 0) // TRI_DIM) == (iota((C, C), 1) // TRI_DIM)
-    lines_out = []
-    for line in range(lines):
-        rows = slice(line * tokens, (line + 1) * tokens)
-        query = feature(query_key[rows, :C]).astype(BF16)
-        key = jnp.where(valid, feature(query_key[rows, C:]), 0.0).astype(BF16)
-        values = value_gate[rows, :C].astype(BF16)
-        state = jnp.where(same_head, mm_tn(key, values) * scale, 0.0).astype(BF16)
-        update = (sigmoid(value_gate[rows, C:]) * mm(query, state)).astype(BF16)
-        lines_out.append(x[rows] + mm(update, out))
-    return lines_out
+    return valid, same_head
 
 
 def row_kernel(scale, n_col, lines, mask_ref, gain_ref, qk_ref, vg_ref, out_w_ref, own_ref, *refs):
@@ -105,15 +113,19 @@
             rows = slice(line * block, (line + 1) * block)
             piece = pieces[k - 1][rows, :] if k else own_ref[rows, :]
             x_scr[pl.ds(start, block), :] = piece.astype(F32)
-    length = jnp.sum(mask_ref[...])
-    done = triangle(
-        x_scr[...], lines, length, gain_ref[0:1, :], qk_ref[0], vg_ref[0], out_w_ref[0], scale
-    )
-    for line in range(lines):
-        z_scr[line * tokens : (line + 1) * tokens, :] = done[line]
+    valid, same_head = masks(tokens, mask_ref)
     owners, per_owner, _ = z_ref.shape
+    per_line = per_owner // lines
+    for first in range(0, lines, GROUP):
+        group = [x_scr[line * tokens : (line + 1) * tokens, :] for line in range(first, first + GROUP)]
+        group = triangle_lines(group, valid, same_head, gain_ref[0:1, :], qk_ref[0], vg_ref[0], out_w_ref[0], scale)
+        for n, z in enumerate(group):
+            for m in range(per_line):
+                for o in range(owners // 8):
+                    base = 8 * (o * per_owner + (first + n) * per_line + m)
+                    z_scr[base : base + 8, :] = z[m * owners + o * 8 :][:8]
     for d in range(owners):
-        z_ref[d] = z_scr[pl.ds(d, per_owner, stride=owners), :].astype(BF16)
+        z_ref[d] = z_scr[pl.ds(d // 8 * 8 * per_owner + d % 8, per_owner, stride=8), :].astype(BF16)
 
 
 def bias_form(row_count, lines, heads_here):
@@ -129,11 +141,14 @@
     tokens = n_row * row_count
     devices = n_row * n_col
     z_scr[...] = z_ref[...].astype(F32)
-    x = jnp.concatenate([z_scr[pl.ds(line, tokens, stride=lines), :] for line in range(lines)], axis=0)
-    length = jnp.sum(mask_ref[...])
-    done = triangle(x, lines, length, gain_ref[1:2, :], qk_ref[1], vg_ref[1], out_w_ref[1], scale)
-    done = [part.astype(BF16).astype(F32) for part in done]
-    normed = [layer_norm(part, bias_gain_ref[...]).astype(BF16) for part in done]
+    valid, same_head = masks(tokens, mask_ref)
+    done, normed = [], []
+    for first in range(0, lines, GROUP):
+        group = [z_scr[pl.ds(line, tokens, stride=lines), :] for line in range(first, first + GROUP)]
+        group = triangle_lines(group, valid, same_head, gain_ref[1:2, :], qk_ref[1], vg_ref[1], out_w_ref[1], scale)
+        for x in group:
+            done.append(x.astype(BF16).astype(F32))
+            normed.append(layer_norm(done[-1], bias_gain_ref[...]).astype(BF16))
     side, deep = bias_form(row_count, lines, heads_here)
     chunk = row_count + deep
     proj = bias_proj_ref[...].astype(F32)
@@ -164,30 +179,27 @@
         copy.wait()
 
 
-def kv_kernel(count, single_ref, gain_ref, wk_ref, wv_ref, x_ref, *refs):
-    rest, (kv_ref, normed_ref, own_ref), rest_out, sems = (
-        refs[:count], refs[count : count + 3], refs[count + 3 : -1], refs[-1],
-    )
-    copies = start_all([(x_ref.at[lax.axis_index("col")], own_ref), *zip(rest, rest_out)], sems)
-    gain = gain_ref[...]
+def kv_kernel(count, single_ref, gain_ref, qk_ref, vg_ref, x_ref, *refs):
+    rest, (kv_ref, normed_ref, own_ref), rest_out, (single, gain, wk, wv, sems) = (
+        refs[:count], refs[count : count + 3], refs[count + 3 : -5], refs[-5:],
+    )
+    pairs = [(single_ref, single), (gain_ref, gain), (qk_ref.at[1], wk), (vg_ref.at[0], wv)]
+    pairs += [(x_ref.at[lax.axis_index("col")], own_ref), *zip(rest, rest_out)]
+    copies = start_all(pairs, sems)
+    wait_all(copies[:2])
     gains = jnp.concatenate([gain[c : c + 1, :] for c in range(gain.shape[0])], axis=1)
-    normed = layer_norm(single_ref[...].astype(F32), gains).astype(BF16)
+    normed = layer_norm(single[...].astype(F32), gains).astype(BF16)
     normed_ref[...] = normed
-    kv_ref[0] = mm_nt(normed, wk_ref[...]).astype(BF16)
-    kv_ref[1] = mm_nt(normed, wv_ref[...]).astype(BF16)
-    wait_all(copies)
-
-
-def qg_kernel(count, normed_ref, qk_ref, vg_ref, *refs):
-    rest, (q_ref, g_ref), rest_out, (wq, wg, sems) = (
-        refs[:count], refs[count : count + 2], refs[count + 2 : -3], refs[-3:],
-    )
-    copies = start_all([(qk_ref.at[0], wq), (vg_ref.at[1], wg), *zip(rest, rest_out)], sems)
-    copies[0].wait()
-    q_ref[...] = mm_nt(normed_ref[...], wq[...]).astype(BF16)
-    copies[1].wait()
-    g_ref[...] = mm_nt(normed_ref[...], wg[...])
-    wait_all(copies[2:])
+    copies[2].wait()
+    kv_ref[0] = mm_nt(normed, wk[...]).astype(BF16)
+    copies[3].wait()
+    kv_ref[1] = mm_nt(normed, wv[...]).astype(BF16)
+    wait_all(copies[4:])
+
+
+def qg_kernel(normed_ref, qk_ref, vg_ref, q_ref, g_ref):
+    q_ref[...] = mm_nt(normed_ref[...], qk_ref[0]).astype(BF16)
+    g_ref[...] = mm_nt(normed_ref[...], vg_ref[1])
 
 
 def attn_kernel(
@@ -263,12 +275,9 @@
         out_ref[i] = scr[pl.ds(i, out_ref.shape[1], stride=chunk), :].astype(BF16)
 
 
-def pick_kernel(n_col, x_ref, single_ref, gain_ref, qk_ref, vg_ref, *refs):
-    sent, (single_out, gain_out, wk_out, wv_out, sems) = refs[: n_col - 1], refs[n_col - 1 :]
+def pick_kernel(n_col, x_ref, *refs):
     me = lax.axis_index("col")
-    pairs = [(x_ref.at[me ^ (k + 1)], sent[k]) for k in range(n_col - 1)]
-    pairs += [(qk_ref.at[1], wk_out), (vg_ref.at[0], wv_out), (single_ref, single_out), (gain_ref, gain_out)]
-    wait_all(start_all(pairs, sems))
+    wait_all(start_all([(x_ref.at[me ^ (k + 1)], refs[k]) for k in range(n_col - 1)], refs[-1]))
 
 
 def swap_col(blocks, n_col):
@@ -299,22 +308,26 @@
 
     blocks = pair_act.reshape(n_col, own_rows * col_count, C)
     block = pltpu.VMEM(blocks.shape[1:], BF16)
-    gain2 = attn_gain.reshape(-1, C)
+    picked = call(
+        functools.partial(pick_kernel, n_col), [block] * (n_col - 1),
+        [], [], [blocks], [pltpu.SemaphoreType.DMA((n_col - 1,))],
+    )
+    pieces = swap_col(picked, n_col)
     wqk, wvg = attn_qk.swapaxes(1, 2), attn_vg.swapaxes(1, 2)
     weight = pltpu.VMEM(wqk.shape[1:], BF16)
-    *picked, single, gain2, wk, wv = call(
-        functools.partial(pick_kernel, n_col),
-        [block] * (n_col - 1) + [chip(single), chip(gain2), weight, weight],
-        [], [], [blocks, single, gain2, wqk, wvg], [pltpu.SemaphoreType.DMA((n_col + 3,))],
-    )
-    pieces = swap_col(picked, n_col)
-    early = [token_mask.reshape(1, tokens), tri_gain, tri_qk, tri_vg, tri_out]
-    kv, normed, own, *early = call(
-        functools.partial(kv_kernel, len(early)),
-        [pltpu.VMEM((2, row_count, width), BF16), chip(single), block, *map(chip, early)],
-        [], [single, gain2, wk, wv], [blocks, *early], [pltpu.SemaphoreType.DMA((1 + len(early),))],
-    )
-    mask, tri_gain, tri_qk, tri_vg, tri_out = early
+    gain2 = attn_gain.reshape(-1, C)
+    rest = [
+        token_mask.reshape(1, tokens), tri_gain, tri_qk, tri_vg, tri_out, bias_gain.reshape(1, C), bias_proj.T,
+        chain_bias.reshape(1, -1), pos_slope.reshape(1, -1), chain_index.reshape(1, tokens),
+        residue_index.reshape(1, tokens),
+    ]
+    kv, normed, own, *rest = call(
+        functools.partial(kv_kernel, len(rest)),
+        [pltpu.VMEM((2, row_count, width), BF16), chip(single), block, *map(chip, rest)],
+        [], [], [single, gain2, wqk, wvg, blocks, *rest],
+        [chip(single), chip(gain2), weight, weight, pltpu.SemaphoreType.DMA((5 + len(rest),))],
+    )
+    mask, tri_gain, tri_qk, tri_vg, tri_out, bias_gain, bias_proj, chain_bias, pos_slope, chain, residue = rest
     z_out = call(
         functools.partial(row_kernel, scale, n_col, own_rows),
         pltpu.VMEM((devices, own_rows * own_cols, C), BF16),
@@ -323,16 +336,10 @@
     )
 
     z_in = lax.all_to_all(z_out, ("row", "col"), 0, 0, tiled=True)
-    late = [
-        bias_gain.reshape(1, C), bias_proj.T, chain_bias.reshape(1, -1), pos_slope.reshape(1, -1),
-        chain_index.reshape(1, tokens), residue_index.reshape(1, tokens), attn_out,
-    ]
-    query, gate, *late = call(
-        functools.partial(qg_kernel, len(late)),
-        [pltpu.VMEM((row_count, width), BF16), pltpu.VMEM((row_count, width), F32), *map(chip, late)],
-        [], [normed], [wqk, wvg, *late], [weight, weight, pltpu.SemaphoreType.DMA((2 + len(late),))],
-    )
-    bias_gain, bias_proj, chain_bias, pos_slope, chain, residue, attn_out = late
+    query, gate = call(
+        qg_kernel, [pltpu.VMEM((row_count, width), BF16), pltpu.VMEM((row_count, width), F32)],
+        [], [normed, wqk, wvg],
+    )
     back = call(
         functools.partial(col_kernel, scale, n_row, n_col, row_count, col_count, heads_here),
         pltpu.VMEM((devices * chunk, C), BF16),
@@ -343,14 +350,21 @@
         ],
         scratch=[pltpu.VMEM((own_cols * tokens, C), F32), pltpu.VMEM((devices * chunk, C), F32)],
     )
+    def kv_from(sent, step):
+        return lax.ppermute(sent, "row", [(i, i ^ step) for i in range(n_row)])
+
+    held, slots = [kv[None]], [0]
+    if n_row > 1:
+        held.append(kv_from(held[0], 1))
+        slots.append(1)
+    if n_row > 2:
+        both = jnp.concatenate(held, axis=0)
+        for step in range(2, n_row, 2):
+            held.append(kv_from(both, step))
+            slots += [step, step ^ 1]
+    back, held = lax.optimization_barrier((back, held))
     got = lax.all_to_all(back.reshape(devices, chunk // 2, 2, C), ("row", "col"), 0, 0, tiled=True)
     got = got.reshape(devices * chunk, C)
-
-    held, slots = [kv[None]], [0]
-    for step in kv_steps(n_row):
-        sent = held[0] if len(held) == 1 else jnp.concatenate(held, axis=0)
-        held.append(lax.ppermute(sent, "row", [(i, i ^ step) for i in range(n_row)]))
-        slots += [slot ^ step for slot in slots]
 
     terms = call(
         functools.partial(attn_kernel, n_row, n_col, row_count, heads_here, slots),
@@ -371,10 +385,6 @@
         [], [mine], scratch=[pltpu.VMEM((col_count * chunk, C), F32)],
     )
     return (pair_out, token_update)
-
-
-def kv_steps(n_row):
-    return [1 << b for b in range((n_row - 1).bit_length())]
 
 
 def solution(mesh):

time: 46.9 us -> 45.6 us (0.972)
  Pallas kernels: 10.1 us -> 8.09 us
  waiting for transfers between devices: 14.9 us -> 16.5 us
  starting transfers between devices: 20.2 us -> 19.4 us
    all_to_all x1, waiting for transfers between devices: 0.01 us -> 8.13 us  [on_device(): lax.all_to_all(back.reshape(devices, chunk // 2, 2, C), ('row', 'col'), 0...]
    all_to_all x1, waiting for transfers between devices: 4.77 us -> 0.01 us  [on_device(): z_in = lax.all_to_all(z_out, ('row', 'col'), 0, 0, tiled=True)]
    pallas_call x7, Pallas kernels: 10.1 us -> 8.09 us  [call(): pl.pallas_call(kernel, out_shape=out_shape, in_specs=[SMEM] * len(smem) +...]
    ppermute x6, waiting for transfers between devices: 4.08 us -> 2.97 us  [swap_col(): got.append(lax.ppermute(block, 'col', [(i, i ^ k) for i in range(n_col)]))]
    ppermute x3 -> x4, starting transfers between devices: 7.33 us -> 6.53 us  [kv_from(): return lax.ppermute(sent, 'row', [(i, i ^ step) for i in range(n_row)])]
    ppermute x3 -> x4, waiting for transfers between devices: 6.07 us -> 5.39 us  [kv_from(): return lax.ppermute(sent, 'row', [(i, i ^ step) for i in range(n_row)])]
  transfers between devices with their start and end apart: 11 -> 12, of which waited for: 7 -> 6; matrix products, arithmetic and copies ran while one was open for 0% -> 0% of each run, Pallas kernels for 13% -> 11%
where the time goes in v3:
time: 45.6 us; the launch traced here: 45.3 us
  starting transfers between devices  19.4 us (43%)
  waiting for transfers between devices  16.5 us (36%)
  Pallas kernels  8.09 us (18%)
  between operations  0.71 us (2%)
  other arithmetic  0.62 us (1%)
    all_to_all x1, waiting for transfers between devices, on_device(): lax.all_to_all(back.reshape(devices, chunk // 2, 2, C), ('row', 'col'), 0...  8.13 us
    pallas_call x7, Pallas kernels, call(): pl.pallas_call(kernel, out_shape=out_shape, in_specs=[SMEM] * len(smem) +...  8.09 us
    ppermute x4, starting transfers between devices, kv_from(): return lax.ppermute(sent, 'row', [(i, i ^ step) for i in range(n_row)])  6.53 us
    ppermute x4, waiting for transfers between devices, kv_from(): return lax.ppermute(sent, 'row', [(i, i ^ step) for i in range(n_row)])  5.39 us
    all_to_all x1, starting transfers between devices, on_device(): z_in = lax.all_to_all(z_out, ('row', 'col'), 0, 0, tiled=True)  5.23 us
    ppermute x6, starting transfers between devices, swap_col(): got.append(lax.ppermute(block, 'col', [(i, i ^ k) for i in range(n_col)]))  5.08 us
    ppermute x6, waiting for transfers between devices, swap_col(): got.append(lax.ppermute(block, 'col', [(i, i ^ k) for i in range(n_col)]))  2.97 us
    all_to_all x1, starting transfers between devices, on_device(): lax.all_to_all(back.reshape(devices, chunk // 2, 2, C), ('row', 'col'), 0...  2.58 us
  transfers between devices with their start and end apart: 12, of which 6 were waited for; matrix products, arithmetic and copies ran while one was open for 0% of the time, Pallas kernels for 11%

profile of v3, /device:TPU:0, one launch (start us, length us, event | category | flops | bytes accessed | tf_op | source)
XLA Modules:
  0.0 45.3 jit_solution(12423019894258997585)
XLA Ops:
  0.6 0.8 %shard_map.177 = (bf16[128,128]{1,0:T(8,128)(2,1)S(1)}, bf16[128,128]{1,0:T(8,128)(2,1)S(1)}, bf16[128,128]{1,0:T(8,128)(2,1)S(1)}) custom-call(bf16[4,128,128]{2,1,0:T(8,128)(2,1)} %bitcast.25), custom_call_target="tpu_custom_call" | custom-call | tf_op jit(solution)/shard_map/pallas_call | solution.py:34
  1.5 0.6 %collective-permute-start = (bf16[128,128]{1,0:T(8,128)(2,1)S(1)}, bf16[128,128]{1,0:T(8,128)(2,1)S(1)}, u32[]{:S(2)}, u32[]{:S(2)}) collective-permute-start(bf16[128,128]{1,0:T(8,128)(2,1)S(1)} %get-tuple-element.39), channel_id=1, source_target_pairs={{0,1},{1,0},{2,3},{3,2},{4,5},{5,4},{6,7},{7,6},{8,9},{9,8},{10,11... | collective-permute-start | bytes 98312 | tf_op jit(solution)/shard_map/ppermute | solution.py:286
  2.0 2.6 %collective-permute-start.1 = (bf16[128,128]{1,0:T(8,128)(2,1)S(1)}, bf16[128,128]{1,0:T(8,128)(2,1)S(1)}, u32[]{:S(2)}, u32[]{:S(2)}) collective-permute-start(bf16[128,128]{1,0:T(8,128)(2,1)S(1)} %get-tuple-element.40), channel_id=1, source_target_pairs={{0,2},{1,3},{2,0},{3,1},{4,6},{5,7},{6,4},{7,5},{8,10},{9,11},{10,... | collective-permute-start | bytes 98312 | tf_op jit(solution)/shard_map/ppermute | solution.py:286
  4.6 0.0 collective-permute-start.2
  4.6 1.7 %shard_map.176 = (bf16[2,16,192]{2,1,0:T(8,128)(2,1)S(1)}, bf16[16,768]{1,0:T(8,128)(2,1)S(1)}, bf16[128,128]{1,0:T(8,128)(2,1)S(1)}, s32[1,128]{1,0:T(1,128)S(1...) custom-call(bf16[16,768]{1,0:T(8,128)(2,1)} %single_ref.1, ...), custom_call_target="tpu_custom_call" | custom-call | tf_op jit(solution)/shard_map/pallas_call | solution.py:34
  6.3 0.0 collective-permute-done.refs_0_
  6.3 0.2 collective-permute-done.1.refs_1_
  6.6 1.4 %collective-permute-done.2.refs_2_ = bf16[128,128]{1,0:T(8,128)(2,1)S(1)} collective-permute-done((bf16[128,128]{1,0:T(8,128)(2,1)S(1)}, bf16[128,128]{1,0:T(8,128)(2,1)S(1)}, u32[]{:S(2)}, u32[]{:S(2)}) %collective-permute-start.2) | collective-permute-done | bytes 32800 | tf_op jit(solution)/shard_map/ppermute | solution.py:286
  7.9 1.7 %shard_map.178 = bf16[32,16,128]{2,1,0:T(8,128)(2,1)} custom-call(s32[1,128]{1,0:T(1,128)S(1)} %get-tuple-element.31.mask_ref, f32[2,128]{1,0:T(2,128)S(1)} %get-tuple-element.32.gain_ref, bf16[2,128,256]{2,1,0:T(8,128)(2,1)S(1)} %get-tuple-element.33.qk_ref, bf16[2,128,256]{2,1,0:T(8,128)(2,1)S(1)} %get-tuple-element.34.vg_ref, ...), custom_call_target="tpu_custom_call" | custom-call | tf_op jit(solution)/shard_map/pallas_call | solution.py:34
  9.6 0.0 copy-start
  9.6 0.0 copy-start.1
  9.6 5.2 %all-to-all-start = ((bf16[32,16,128]{2,1,0:T(8,128)(2,1)}), bf16[32,16,128]{2,1,0:T(8,128)(2,1)S(1)}, u32[]{:S(2)}, u32[]{:S(2)}) async-start(bf16[32,16,128]{2,1,0:T(8,128)(2,1)} %shard_map.178), calls=%async_computation | async-start | bytes 262144 | tf_op jit(solution)/shard_map/all_to_all | solution.py:338
  14.9 1.8 %collective-permute-start.3 = (bf16[1,2,16,192]{3,2,1,0:T(8,128)(2,1)S(1)}, bf16[1,2,16,192]{3,2,1,0:T(8,128)(2,1)S(1)}, u32[]{:S(2)}, u32[]{:S(2)}) collective-permute-start(bf16[1,2,16,192]{3,2,1,0:T(8,128)(2,1)S(1)} %bitcast.22), channel_id=1, source_target_pairs={{0,4},{4,0},{8,12},{12,8},{16,20},{20,16},{24,28},{28,24},{1,5},{5... | collective-permute-start | bytes 36872 | tf_op jit(solution)/shard_map/ppermute | solution.py:354
  16.7 2.0 %collective-permute-done.3.refs_1_ = bf16[1,2,16,192]{3,2,1,0:T(8,128)(2,1)S(1)} collective-permute-done((bf16[1,2,16,192]{3,2,1,0:T(8,128)(2,1)S(1)}, bf16[1,2,16,192]{3,2,1,0:T(8,128)(2,1)S(1)}, u32[]{:S(2)}, u32[]{:S(2)}) %collective-permute-start.3) | collective-permute-done | bytes 12320 | tf_op jit(solution)/shard_map/ppermute | solution.py:354
  18.7 2.1 %collective-permute-start.4 = (bf16[2,2,16,192]{3,2,1,0:T(8,128)(2,1)S(1)}, bf16[2,2,16,192]{3,2,1,0:T(8,128)(2,1)S(1)}, u32[]{:S(2)}, u32[]{:S(2)}) collective-permute-start(bf16[2,2,16,192]{3,2,1,0:T(8,128)(2,1)S(1)} %pad_maximum_fusion), channel_id=1, source_target_pairs={{0,8},{4,12},{8,0},{12,4},{16,24},{20,28},{24,16},{28,20},{1,9},{5... | collective-permute-start | bytes 73736 | tf_op jit(solution)/shard_map/ppermute | solution.py:354
  20.8 2.6 %collective-permute-start.5 = (bf16[2,2,16,192]{3,2,1,0:T(8,128)(2,1)S(1)}, bf16[2,2,16,192]{3,2,1,0:T(8,128)(2,1)S(1)}, u32[]{:S(2)}, u32[]{:S(2)}) collective-permute-start(bf16[2,2,16,192]{3,2,1,0:T(8,128)(2,1)S(1)} %pad_maximum_fusion), channel_id=1, source_target_pairs={{0,16},{4,20},{8,24},{12,28},{16,0},{20,4},{24,8},{28,12},{1,17},{... | collective-permute-start | bytes 73736 | tf_op jit(solution)/shard_map/ppermute | solution.py:354
  23.4 0.0 collective-permute-start.6
  23.4 0.0 all-to-all-done
  23.4 2.3 %shard_map.179 = bf16[576,128]{1,0:T(8,128)(2,1)} custom-call(s32[1,128]{1,0:T(1,128)S(1)} %get-tuple-element.31.mask_ref, f32[2,128]{1,0:T(2,128)S(1)} %get-tuple-element.32.gain_ref, bf16[2,128,256]{2,1,0:T(8,128)(2,1)S(1)} %get-tuple-element.33.qk_ref, bf16[2,128,256]{2,1,0:T(8,128)(2,1)S(1)} %get-tuple-element.34.vg_ref, ...), custom_call_target="tpu_custom_call" | custom-call | tf_op jit(solution)/shard_map/pallas_call | solution.py:34
  25.7 0.0 collective-permute-done.4.refs_2_
  25.7 0.0 collective-permute-done.5.refs_3_
  25.7 3.4 %collective-permute-done.6.refs_4_ = bf16[2,2,16,192]{3,2,1,0:T(8,128)(2,1)S(1)} collective-permute-done((bf16[2,2,16,192]{3,2,1,0:T(8,128)(2,1)S(1)}, bf16[2,2,16,192]{3,2,1,0:T(8,128)(2,1)S(1)}, u32[]{:S(2)}, u32[]{:S(2)}) %collective-permute-start.6) | collective-permute-done | bytes 24608 | tf_op jit(solution)/shard_map/ppermute | solution.py:354
  29.1 2.6 %all-to-all-start.1 = ((bf16[32,9,2,128]{3,2,1,0:T(2,128)(2,1)}), bf16[32,9,2,128]{3,2,1,0:T(2,128)(2,1)S(1)}, u32[]{:S(2)}, u32[]{:S(2)}) async-start(bf16[32,9,2,128]{3,2,1,0:T(2,128)(2,1)} %bitcast.13), calls=%async_computation.1 | async-start | bytes 294912 | tf_op jit(solution)/shard_map/all_to_all | solution.py:366
  31.7 0.0 copy-done
  31.7 0.0 copy-done.1
  31.7 0.0 copy-start.2
  31.7 0.3 shard_map.181
  32.0 8.1 %all-to-all-done.1 = bf16[32,9,2,128]{3,2,1,0:T(2,128)(2,1)S(1)} async-done(((bf16[32,9,2,128]{3,2,1,0:T(2,128)(2,1)}), bf16[32,9,2,128]{3,2,1,0:T(2,128)(2,1)S(1)}, u32[]{:S(2)}, u32[]{:S(2)}) %all-to-all-start.1) | async-done | bytes 147488 | tf_op jit(solution)/shard_map/all_to_all | solution.py:366
  40.1 0.0 copy-done.2
  40.1 0.6 %shard_map.182 = (bf16[16,192]{1,0:T(8,128)(2,1)S(1)}, bf16[16,192]{1,0:T(8,128)(2,1)S(1)}, bf16[16,192]{1,0:T(8,128)(2,1)S(1)}, bf16[16,192]{1,0:T(8,128)(2,1)S(1)}) custom-call(f32[1,4]{1,0:T(1,128)S(1)} %get-tuple-element.44.chain_bias_ref, f32[1,4]{1,0:T(1,128)S(1)} %get-tuple-element.45.slope_ref, s32[1,128]{1,0:T(1,128)S(1)} %get-tuple-element.31.mask_ref, ...), custom_call_target="tpu_custom_call" | custom-call | tf_op jit(solution)/shard_map/pallas_call | solution.py:34
  40.7 0.3 collective-permute-start.7
  41.1 0.3 collective-permute-start.8
  41.4 1.3 %collective-permute-start.9 = (bf16[16,192]{1,0:T(8,128)(2,1)S(1)}, bf16[16,192]{1,0:T(8,128)(2,1)S(1)}, u32[]{:S(2)}, u32[]{:S(2)}) collective-permute-start(bf16[16,192]{1,0:T(8,128)(2,1)S(1)} %get-tuple-element.59), channel_id=1, source_target_pairs={{0,3},{1,2},{2,1},{3,0},{4,7},{5,6},{6,5},{7,4},{8,11},{9,10},{10,... | collective-permute-start | bytes 18440 | tf_op jit(solution)/shard_map/ppermute | solution.py:286
  42.7 0.7 %shard_map.180 = bf16[16,32,128]{2,1,0:T(8,128)(2,1)} custom-call(bf16[576,128]{1,0:T(8,128)(2,1)S(1)} %bitcast.20), custom_call_target="tpu_custom_call" | custom-call | tf_op jit(solution)/shard_map/pallas_call | solution.py:34
  43.4 0.0 collective-permute-done.7
  43.4 1.4 %collective-permute-done.8 = bf16[16,192]{1,0:T(8,128)(2,1)S(1)} collective-permute-done((bf16[16,192]{1,0:T(8,128)(2,1)S(1)}, bf16[16,192]{1,0:T(8,128)(2,1)S(1)}, u32[]{:S(2)}, u32[]{:S(2)}) %collective-permute-start.8) | collective-permute-done | bytes 6176 | tf_op jit(solution)/shard_map/ppermute | solution.py:286
  44.7 0.0 collective-permute-done.9
  44.7 0.6 %add_convert_fusion = bf16[16,192]{1,0:T(8,128)(2,1)} fusion(bf16[16,192]{1,0:T(8,128)(2,1)S(1)} %collective-permute-done.9, bf16[16,192]{1,0:T(8,128)(2,1)S(1)} %collective-permute-done.8, bf16[16,192]{1,0:T(8,128)(2,1)S(1)} %collective-permute-done.7, bf16[16,192]{1,0:T(8,128)(2,1)S(1)} %get-tuple-element.56), kind=kLoop, calls=%fused_computation.1 | loop fusion | flops 24576 | bytes 30720 | tf_op jit(solution)/shard_map/convert_element_type | solution.py:378
  (1 shorter events, 0.0 us)
Async XLA Ops:
  1.5 4.9 %collective-permute-start = (bf16[128,128]{1,0:T(8,128)(2,1)S(1)}, bf16[128,128]{1,0:T(8,128)(2,1)S(1)}, u32[]{:S(2)}, u32[]{:S(2)}) collective-permute-start(bf16[128,128]{1,0:T(8,128)(2,1)S(1)} %get-tuple-element.39), channel_id=1, source_target_pairs={{0,1},{1,0},{2,3},{3,2},{4,5},{5,4},{6,7},{7,6},{8,9},{9,8},{10,11... | collective-permute-start | bytes 98312 | tf_op jit(solution)/shard_map/ppermute | solution.py:286
  2.0 4.5 %collective-permute-start.1 = (bf16[128,128]{1,0:T(8,128)(2,1)S(1)}, bf16[128,128]{1,0:T(8,128)(2,1)S(1)}, u32[]{:S(2)}, u32[]{:S(2)}) collective-permute-start(bf16[128,128]{1,0:T(8,128)(2,1)S(1)} %get-tuple-element.40), channel_id=1, source_target_pairs={{0,2},{1,3},{2,0},{3,1},{4,6},{5,7},{6,4},{7,5},{8,10},{9,11},{10,... | collective-permute-start | bytes 98312 | tf_op jit(solution)/shard_map/ppermute | solution.py:286
  4.6 3.4 %collective-permute-start.2 = (bf16[128,128]{1,0:T(8,128)(2,1)S(1)}, bf16[128,128]{1,0:T(8,128)(2,1)S(1)}, u32[]{:S(2)}, u32[]{:S(2)}) collective-permute-start(bf16[128,128]{1,0:T(8,128)(2,1)S(1)} %get-tuple-element.41), channel_id=1, source_target_pairs={{0,3},{1,2},{2,1},{3,0},{4,7},{5,6},{6,5},{7,4},{8,11},{9,10},{10,... | collective-permute-start | bytes 98312 | tf_op jit(solution)/shard_map/ppermute | solution.py:286
  9.6 22.1 %copy-start = (bf16[2,768,192]{1,2,0:T(8,128)(2,1)S(1)}, bf16[2,768,192]{1,2,0:T(8,128)(2,1)}, u32[]{:S(2)}) copy-start(bf16[2,768,192]{1,2,0:T(8,128)(2,1)} %param.31) | copy-start | bytes 1769476
  9.6 22.1 %copy-start.1 = (bf16[2,768,192]{1,2,0:T(8,128)(2,1)S(1)}, bf16[2,768,192]{1,2,0:T(8,128)(2,1)}, u32[]{:S(2)}) copy-start(bf16[2,768,192]{1,2,0:T(8,128)(2,1)} %param.32) | copy-start | bytes 1769476
  9.6 13.8 %all-to-all-start = ((bf16[32,16,128]{2,1,0:T(8,128)(2,1)}), bf16[32,16,128]{2,1,0:T(8,128)(2,1)S(1)}, u32[]{:S(2)}, u32[]{:S(2)}) async-start(bf16[32,16,128]{2,1,0:T(8,128)(2,1)} %shard_map.178), calls=%async_computation | async-start | bytes 262144 | tf_op jit(solution)/shard_map/all_to_all | solution.py:338
  14.9 3.8 %collective-permute-start.3 = (bf16[1,2,16,192]{3,2,1,0:T(8,128)(2,1)S(1)}, bf16[1,2,16,192]{3,2,1,0:T(8,128)(2,1)S(1)}, u32[]{:S(2)}, u32[]{:S(2)}) collective-permute-start(bf16[1,2,16,192]{3,2,1,0:T(8,128)(2,1)S(1)} %bitcast.22), channel_id=1, source_target_pairs={{0,4},{4,0},{8,12},{12,8},{16,20},{20,16},{24,28},{28,24},{1,5},{5... | collective-permute-start | bytes 36872 | tf_op jit(solution)/shard_map/ppermute | solution.py:354
  18.7 7.0 %collective-permute-start.4 = (bf16[2,2,16,192]{3,2,1,0:T(8,128)(2,1)S(1)}, bf16[2,2,16,192]{3,2,1,0:T(8,128)(2,1)S(1)}, u32[]{:S(2)}, u32[]{:S(2)}) collective-permute-start(bf16[2,2,16,192]{3,2,1,0:T(8,128)(2,1)S(1)} %pad_maximum_fusion), channel_id=1, source_target_pairs={{0,8},{4,12},{8,0},{12,4},{16,24},{20,28},{24,16},{28,20},{1,9},{5... | collective-permute-start | bytes 73736 | tf_op jit(solution)/shard_map/ppermute | solution.py:354
  20.8 4.9 %collective-permute-start.5 = (bf16[2,2,16,192]{3,2,1,0:T(8,128)(2,1)S(1)}, bf16[2,2,16,192]{3,2,1,0:T(8,128)(2,1)S(1)}, u32[]{:S(2)}, u32[]{:S(2)}) collective-permute-start(bf16[2,2,16,192]{3,2,1,0:T(8,128)(2,1)S(1)} %pad_maximum_fusion), channel_id=1, source_target_pairs={{0,16},{4,20},{8,24},{12,28},{16,0},{20,4},{24,8},{28,12},{1,17},{... | collective-permute-start | bytes 73736 | tf_op jit(solution)/shard_map/ppermute | solution.py:354
  23.4 5.7 %collective-permute-start.6 = (bf16[2,2,16,192]{3,2,1,0:T(8,128)(2,1)S(1)}, bf16[2,2,16,192]{3,2,1,0:T(8,128)(2,1)S(1)}, u32[]{:S(2)}, u32[]{:S(2)}) collective-permute-start(bf16[2,2,16,192]{3,2,1,0:T(8,128)(2,1)S(1)} %pad_maximum_fusion), channel_id=1, source_target_pairs={{0,24},{4,28},{8,16},{12,20},{16,8},{20,12},{24,0},{28,4},{1,25},{... | collective-permute-start | bytes 73736 | tf_op jit(solution)/shard_map/ppermute | solution.py:354
  29.1 11.0 %all-to-all-start.1 = ((bf16[32,9,2,128]{3,2,1,0:T(2,128)(2,1)}), bf16[32,9,2,128]{3,2,1,0:T(2,128)(2,1)S(1)}, u32[]{:S(2)}, u32[]{:S(2)}) async-start(bf16[32,9,2,128]{3,2,1,0:T(2,128)(2,1)} %bitcast.13), calls=%async_computation.1 | async-start | bytes 294912 | tf_op jit(solution)/shard_map/all_to_all | solution.py:366
  31.7 8.4 %copy-start.2 = (bf16[192,768]{1,0:T(8,128)(2,1)S(1)}, bf16[192,768]{1,0:T(8,128)(2,1)}, u32[]{:S(2)}) copy-start(bf16[192,768]{1,0:T(8,128)(2,1)} %out_w_ref.1) | copy-start | bytes 884740
  40.7 2.6 %collective-permute-start.7 = (bf16[16,192]{1,0:T(8,128)(2,1)S(1)}, bf16[16,192]{1,0:T(8,128)(2,1)S(1)}, u32[]{:S(2)}, u32[]{:S(2)}) collective-permute-start(bf16[16,192]{1,0:T(8,128)(2,1)S(1)} %get-tuple-element.57), channel_id=1, source_target_pairs={{0,1},{1,0},{2,3},{3,2},{4,5},{5,4},{6,7},{7,6},{8,9},{9,8},{10,11... | collective-permute-start | bytes 18440 | tf_op jit(solution)/shard_map/ppermute | solution.py:286
  41.1 3.7 %collective-permute-start.8 = (bf16[16,192]{1,0:T(8,128)(2,1)S(1)}, bf16[16,192]{1,0:T(8,128)(2,1)S(1)}, u32[]{:S(2)}, u32[]{:S(2)}) collective-permute-start(bf16[16,192]{1,0:T(8,128)(2,1)S(1)} %get-tuple-element.58), channel_id=1, source_target_pairs={{0,2},{1,3},{2,0},{3,1},{4,6},{5,7},{6,4},{7,5},{8,10},{9,11},{10,... | collective-permute-start | bytes 18440 | tf_op jit(solution)/shard_map/ppermute | solution.py:286
  41.4 3.3 %collective-permute-start.9 = (bf16[16,192]{1,0:T(8,128)(2,1)S(1)}, bf16[16,192]{1,0:T(8,128)(2,1)S(1)}, u32[]{:S(2)}, u32[]{:S(2)}) collective-permute-start(bf16[16,192]{1,0:T(8,128)(2,1)S(1)} %get-tuple-element.59), channel_id=1, source_target_pairs={{0,3},{1,2},{2,1},{3,0},{4,7},{5,6},{6,5},{7,4},{8,11},{9,10},{10,... | collective-permute-start | bytes 18440 | tf_op jit(solution)/shard_map/ppermute | solution.py:286

commit v4 on v3

--- a/solution.py
+++ b/solution.py
@@ -71,7 +71,7 @@
 
 
 def sigmoid(x):
-    return 0.5 * jnp.tanh(0.5 * x) + 0.5
+    return jax.nn.sigmoid(x)
 
 
 GROUP = 4
@@ -83,16 +83,15 @@
     normed = layer_norm(x, gain).astype(BF16)
     query_key, value_gate = mm(normed, qk), mm(normed, vg)
     each = [slice(n * tokens, (n + 1) * tokens) for n in range(len(lines))]
-    keys = [jnp.where(valid, feature(query_key[rows, C:]), 0.0).astype(BF16) for rows in each]
-    values = value_gate[:, :C].astype(BF16)
+    keys = [feature(query_key[rows, C:]).astype(BF16) for rows in each]
+    values = jnp.concatenate([jnp.where(valid, value_gate[rows, :C], 0.0).astype(BF16) for rows in each], axis=0)
     states = [
         jnp.where(same_head, mm_tn(key, values[rows]) * scale, 0.0).astype(BF16) for key, rows in zip(keys, each)
     ]
-    queries = feature(query_key[:, :C]).astype(BF16)
-    gate = sigmoid(value_gate[:, C:])
-    mixed = jnp.concatenate([mm(queries[rows], state) for state, rows in zip(states, each)], axis=0)
-    x = x + mm((gate * mixed).astype(BF16), out)
-    return [x[rows] for rows in each]
+    queries = [feature(query_key[rows, :C]).astype(BF16) for rows in each]
+    gates = [sigmoid(value_gate[rows, C:]) for rows in each]
+    mixed = [mm(query, state) for query, state in zip(queries, states)]
+    return [line + mm((gate * mix).astype(BF16), out) for line, gate, mix in zip(lines, gates, mixed)]
 
 
 def masks(tokens, mask_ref):
@@ -335,7 +334,7 @@
         scratch=[pltpu.VMEM((own_rows * tokens, C), F32)] * 2,
     )
 
-    z_in = lax.all_to_all(z_out, ("row", "col"), 0, 0, tiled=True)
+    z_in = lax.all_to_all(z_out.reshape(devices, -1, 2, C), ("row", "col"), 0, 0, tiled=True)
     query, gate = call(
         qg_kernel, [pltpu.VMEM((row_count, width), BF16), pltpu.VMEM((row_count, width), F32)],
         [], [normed, wqk, wvg],

time: 45.6 us -> 45.7 us (level)
  no operation moved by 1% of the time
where the time goes in v4:
time: 45.7 us; the launch traced here: 45.4 us
  starting transfers between devices  19.4 us (42%)
  waiting for transfers between devices  16.5 us (36%)
  Pallas kernels  8.08 us (18%)
  between operations  0.71 us (2%)
  other arithmetic  0.62 us (1%)
    all_to_all x1, waiting for transfers between devices, on_device(): lax.all_to_all(back.reshape(devices, chunk // 2, 2, C), ('row', 'col'), 0...  8.13 us
    pallas_call x7, Pallas kernels, call(): pl.pallas_call(kernel, out_shape=out_shape, in_specs=[SMEM] * len(smem) +...  8.08 us
    ppermute x4, starting transfers between devices, kv_from(): return lax.ppermute(sent, 'row', [(i, i ^ step) for i in range(n_row)])  6.53 us
    ppermute x4, waiting for transfers between devices, kv_from(): return lax.ppermute(sent, 'row', [(i, i ^ step) for i in range(n_row)])  5.45 us
    all_to_all x1, starting transfers between devices, on_device(): lax.all_to_all(z_out.reshape(devices, -1, 2, C), ('row', 'col'), 0, 0, ti...  5.23 us
    ppermute x6, starting transfers between devices, swap_col(): got.append(lax.ppermute(block, 'col', [(i, i ^ k) for i in range(n_col)]))  5.08 us
    ppermute x6, waiting for transfers between devices, swap_col(): got.append(lax.ppermute(block, 'col', [(i, i ^ k) for i in range(n_col)]))  2.97 us
    all_to_all x1, starting transfers between devices, on_device(): lax.all_to_all(back.reshape(devices, chunk // 2, 2, C), ('row', 'col'), 0...  2.58 us
  transfers between devices with their start and end apart: 12, of which 6 were waited for; matrix products, arithmetic and copies ran while one was open for 0% of the time, Pallas kernels for 11%

profile of v4, /device:TPU:0, one launch (start us, length us, event | category | flops | bytes accessed | tf_op | source)
XLA Modules:
  0.0 45.4 jit_solution(3640376764244189776)
XLA Ops:
  0.6 0.8 %shard_map.177 = (bf16[128,128]{1,0:T(8,128)(2,1)S(1)}, bf16[128,128]{1,0:T(8,128)(2,1)S(1)}, bf16[128,128]{1,0:T(8,128)(2,1)S(1)}) custom-call(bf16[4,128,128]{2,1,0:T(8,128)(2,1)} %bitcast.26), custom_call_target="tpu_custom_call" | custom-call | tf_op jit(solution)/shard_map/pallas_call | solution.py:34
  1.5 0.6 %collective-permute-start = (bf16[128,128]{1,0:T(8,128)(2,1)S(1)}, bf16[128,128]{1,0:T(8,128)(2,1)S(1)}, u32[]{:S(2)}, u32[]{:S(2)}) collective-permute-start(bf16[128,128]{1,0:T(8,128)(2,1)S(1)} %get-tuple-element.39), channel_id=1, source_target_pairs={{0,1},{1,0},{2,3},{3,2},{4,5},{5,4},{6,7},{7,6},{8,9},{9,8},{10,11... | collective-permute-start | bytes 98312 | tf_op jit(solution)/shard_map/ppermute | solution.py:285
  2.0 2.6 %collective-permute-start.1 = (bf16[128,128]{1,0:T(8,128)(2,1)S(1)}, bf16[128,128]{1,0:T(8,128)(2,1)S(1)}, u32[]{:S(2)}, u32[]{:S(2)}) collective-permute-start(bf16[128,128]{1,0:T(8,128)(2,1)S(1)} %get-tuple-element.40), channel_id=1, source_target_pairs={{0,2},{1,3},{2,0},{3,1},{4,6},{5,7},{6,4},{7,5},{8,10},{9,11},{10,... | collective-permute-start | bytes 98312 | tf_op jit(solution)/shard_map/ppermute | solution.py:285
  4.6 0.0 collective-permute-start.2
  4.6 1.7 %shard_map.176 = (bf16[2,16,192]{2,1,0:T(8,128)(2,1)S(1)}, bf16[16,768]{1,0:T(8,128)(2,1)S(1)}, bf16[128,128]{1,0:T(8,128)(2,1)S(1)}, s32[1,128]{1,0:T(1,128)S(1...) custom-call(bf16[16,768]{1,0:T(8,128)(2,1)} %single_ref.1, ...), custom_call_target="tpu_custom_call" | custom-call | tf_op jit(solution)/shard_map/pallas_call | solution.py:34
  6.3 0.0 collective-permute-done.refs_0_
  6.3 0.2 collective-permute-done.1.refs_1_
  6.6 1.4 %collective-permute-done.2.refs_2_ = bf16[128,128]{1,0:T(8,128)(2,1)S(1)} collective-permute-done((bf16[128,128]{1,0:T(8,128)(2,1)S(1)}, bf16[128,128]{1,0:T(8,128)(2,1)S(1)}, u32[]{:S(2)}, u32[]{:S(2)}) %collective-permute-start.2) | collective-permute-done | bytes 32800 | tf_op jit(solution)/shard_map/ppermute | solution.py:285
  7.9 1.7 %shard_map.178 = bf16[32,16,128]{2,1,0:T(8,128)(2,1)} custom-call(s32[1,128]{1,0:T(1,128)S(1)} %get-tuple-element.31.mask_ref, f32[2,128]{1,0:T(2,128)S(1)} %get-tuple-element.32.gain_ref, bf16[2,128,256]{2,1,0:T(8,128)(2,1)S(1)} %get-tuple-element.33.qk_ref, bf16[2,128,256]{2,1,0:T(8,128)(2,1)S(1)} %get-tuple-element.34.vg_ref, ...), custom_call_target="tpu_custom_call" | custom-call | tf_op jit(solution)/shard_map/pallas_call | solution.py:34
  9.7 0.0 copy-start
  9.7 0.0 copy-start.1
  9.7 5.2 %all-to-all-start = ((bf16[32,8,2,128]{3,2,1,0:T(2,128)(2,1)}), bf16[32,8,2,128]{3,2,1,0:T(2,128)(2,1)S(1)}, u32[]{:S(2)}, u32[]{:S(2)}) async-start(bf16[32,8,2,128]{3,2,1,0:T(2,128)(2,1)} %bitcast.11), calls=%async_computation | async-start | bytes 262144 | tf_op jit(solution)/shard_map/all_to_all | solution.py:337
  14.9 1.8 %collective-permute-start.3 = (bf16[1,2,16,192]{3,2,1,0:T(8,128)(2,1)S(1)}, bf16[1,2,16,192]{3,2,1,0:T(8,128)(2,1)S(1)}, u32[]{:S(2)}, u32[]{:S(2)}) collective-permute-start(bf16[1,2,16,192]{3,2,1,0:T(8,128)(2,1)S(1)} %bitcast.23), channel_id=1, source_target_pairs={{0,4},{4,0},{8,12},{12,8},{16,20},{20,16},{24,28},{28,24},{1,5},{5... | collective-permute-start | bytes 36872 | tf_op jit(solution)/shard_map/ppermute | solution.py:353
  16.8 2.0 %collective-permute-done.3.refs_1_ = bf16[1,2,16,192]{3,2,1,0:T(8,128)(2,1)S(1)} collective-permute-done((bf16[1,2,16,192]{3,2,1,0:T(8,128)(2,1)S(1)}, bf16[1,2,16,192]{3,2,1,0:T(8,128)(2,1)S(1)}, u32[]{:S(2)}, u32[]{:S(2)}) %collective-permute-start.3) | collective-permute-done | bytes 12320 | tf_op jit(solution)/shard_map/ppermute | solution.py:353
  18.8 2.1 %collective-permute-start.4 = (bf16[2,2,16,192]{3,2,1,0:T(8,128)(2,1)S(1)}, bf16[2,2,16,192]{3,2,1,0:T(8,128)(2,1)S(1)}, u32[]{:S(2)}, u32[]{:S(2)}) collective-permute-start(bf16[2,2,16,192]{3,2,1,0:T(8,128)(2,1)S(1)} %pad_maximum_fusion), channel_id=1, source_target_pairs={{0,8},{4,12},{8,0},{12,4},{16,24},{20,28},{24,16},{28,20},{1,9},{5... | collective-permute-start | bytes 73736 | tf_op jit(solution)/shard_map/ppermute | solution.py:353
  20.9 2.6 %collective-permute-start.5 = (bf16[2,2,16,192]{3,2,1,0:T(8,128)(2,1)S(1)}, bf16[2,2,16,192]{3,2,1,0:T(8,128)(2,1)S(1)}, u32[]{:S(2)}, u32[]{:S(2)}) collective-permute-start(bf16[2,2,16,192]{3,2,1,0:T(8,128)(2,1)S(1)} %pad_maximum_fusion), channel_id=1, source_target_pairs={{0,16},{4,20},{8,24},{12,28},{16,0},{20,4},{24,8},{28,12},{1,17},{... | collective-permute-start | bytes 73736 | tf_op jit(solution)/shard_map/ppermute | solution.py:353
  23.4 0.0 collective-permute-start.6
  23.4 0.0 all-to-all-done
  23.4 2.2 %shard_map.179 = bf16[576,128]{1,0:T(8,128)(2,1)} custom-call(s32[1,128]{1,0:T(1,128)S(1)} %get-tuple-element.31.mask_ref, f32[2,128]{1,0:T(2,128)S(1)} %get-tuple-element.32.gain_ref, bf16[2,128,256]{2,1,0:T(8,128)(2,1)S(1)} %get-tuple-element.33.qk_ref, bf16[2,128,256]{2,1,0:T(8,128)(2,1)S(1)} %get-tuple-element.34.vg_ref, ...), custom_call_target="tpu_custom_call" | custom-call | tf_op jit(solution)/shard_map/pallas_call | solution.py:34
  25.7 0.0 collective-permute-done.4.refs_2_
  25.7 0.0 collective-permute-done.5.refs_3_
  25.7 3.5 %collective-permute-done.6.refs_4_ = bf16[2,2,16,192]{3,2,1,0:T(8,128)(2,1)S(1)} collective-permute-done((bf16[2,2,16,192]{3,2,1,0:T(8,128)(2,1)S(1)}, bf16[2,2,16,192]{3,2,1,0:T(8,128)(2,1)S(1)}, u32[]{:S(2)}, u32[]{:S(2)}) %collective-permute-start.6) | collective-permute-done | bytes 24608 | tf_op jit(solution)/shard_map/ppermute | solution.py:353
  29.2 2.6 %all-to-all-start.1 = ((bf16[32,9,2,128]{3,2,1,0:T(2,128)(2,1)}), bf16[32,9,2,128]{3,2,1,0:T(2,128)(2,1)S(1)}, u32[]{:S(2)}, u32[]{:S(2)}) async-start(bf16[32,9,2,128]{3,2,1,0:T(2,128)(2,1)} %bitcast.14), calls=%async_computation.1 | async-start | bytes 294912 | tf_op jit(solution)/shard_map/all_to_all | solution.py:365
  31.7 0.0 copy-done
  31.8 0.0 copy-done.1
  31.8 0.0 copy-start.2
  31.8 0.3 shard_map.181
  32.0 8.1 %all-to-all-done.1 = bf16[32,9,2,128]{3,2,1,0:T(2,128)(2,1)S(1)} async-done(((bf16[32,9,2,128]{3,2,1,0:T(2,128)(2,1)}), bf16[32,9,2,128]{3,2,1,0:T(2,128)(2,1)S(1)}, u32[]{:S(2)}, u32[]{:S(2)}) %all-to-all-start.1) | async-done | bytes 147488 | tf_op jit(solution)/shard_map/all_to_all | solution.py:365
  40.2 0.0 copy-done.2
  40.2 0.6 %shard_map.182 = (bf16[16,192]{1,0:T(8,128)(2,1)S(1)}, bf16[16,192]{1,0:T(8,128)(2,1)S(1)}, bf16[16,192]{1,0:T(8,128)(2,1)S(1)}, bf16[16,192]{1,0:T(8,128)(2,1)S(1)}) custom-call(f32[1,4]{1,0:T(1,128)S(1)} %get-tuple-element.44.chain_bias_ref, f32[1,4]{1,0:T(1,128)S(1)} %get-tuple-element.45.slope_ref, s32[1,128]{1,0:T(1,128)S(1)} %get-tuple-element.31.mask_ref, ...), custom_call_target="tpu_custom_call" | custom-call | tf_op jit(solution)/shard_map/pallas_call | solution.py:34
  40.8 0.3 collective-permute-start.7
  41.1 0.3 collective-permute-start.8
  41.4 1.3 %collective-permute-start.9 = (bf16[16,192]{1,0:T(8,128)(2,1)S(1)}, bf16[16,192]{1,0:T(8,128)(2,1)S(1)}, u32[]{:S(2)}, u32[]{:S(2)}) collective-permute-start(bf16[16,192]{1,0:T(8,128)(2,1)S(1)} %get-tuple-element.59), channel_id=1, source_target_pairs={{0,3},{1,2},{2,1},{3,0},{4,7},{5,6},{6,5},{7,4},{8,11},{9,10},{10,... | collective-permute-start | bytes 18440 | tf_op jit(solution)/shard_map/ppermute | solution.py:285
  42.7 0.7 %shard_map.180 = bf16[16,32,128]{2,1,0:T(8,128)(2,1)} custom-call(bf16[576,128]{1,0:T(8,128)(2,1)S(1)} %bitcast.21), custom_call_target="tpu_custom_call" | custom-call | tf_op jit(solution)/shard_map/pallas_call | solution.py:34
  43.4 0.0 collective-permute-done.7
  43.4 1.4 %collective-permute-done.8 = bf16[16,192]{1,0:T(8,128)(2,1)S(1)} collective-permute-done((bf16[16,192]{1,0:T(8,128)(2,1)S(1)}, bf16[16,192]{1,0:T(8,128)(2,1)S(1)}, u32[]{:S(2)}, u32[]{:S(2)}) %collective-permute-start.8) | collective-permute-done | bytes 6176 | tf_op jit(solution)/shard_map/ppermute | solution.py:285
  44.8 0.0 collective-permute-done.9
  44.8 0.6 %add_convert_fusion = bf16[16,192]{1,0:T(8,128)(2,1)} fusion(bf16[16,192]{1,0:T(8,128)(2,1)S(1)} %collective-permute-done.9, bf16[16,192]{1,0:T(8,128)(2,1)S(1)} %collective-permute-done.8, bf16[16,192]{1,0:T(8,128)(2,1)S(1)} %collective-permute-done.7, bf16[16,192]{1,0:T(8,128)(2,1)S(1)} %get-tuple-element.56), kind=kLoop, calls=%fused_computation.1 | loop fusion | flops 24576 | bytes 30720 | tf_op jit(solution)/shard_map/convert_element_type | solution.py:377
  (1 shorter events, 0.0 us)
Async XLA Ops:
  1.5 4.9 %collective-permute-start = (bf16[128,128]{1,0:T(8,128)(2,1)S(1)}, bf16[128,128]{1,0:T(8,128)(2,1)S(1)}, u32[]{:S(2)}, u32[]{:S(2)}) collective-permute-start(bf16[128,128]{1,0:T(8,128)(2,1)S(1)} %get-tuple-element.39), channel_id=1, source_target_pairs={{0,1},{1,0},{2,3},{3,2},{4,5},{5,4},{6,7},{7,6},{8,9},{9,8},{10,11... | collective-permute-start | bytes 98312 | tf_op jit(solution)/shard_map/ppermute | solution.py:285
  2.0 4.5 %collective-permute-start.1 = (bf16[128,128]{1,0:T(8,128)(2,1)S(1)}, bf16[128,128]{1,0:T(8,128)(2,1)S(1)}, u32[]{:S(2)}, u32[]{:S(2)}) collective-permute-start(bf16[128,128]{1,0:T(8,128)(2,1)S(1)} %get-tuple-element.40), channel_id=1, source_target_pairs={{0,2},{1,3},{2,0},{3,1},{4,6},{5,7},{6,4},{7,5},{8,10},{9,11},{10,... | collective-permute-start | bytes 98312 | tf_op jit(solution)/shard_map/ppermute | solution.py:285
  4.6 3.4 %collective-permute-start.2 = (bf16[128,128]{1,0:T(8,128)(2,1)S(1)}, bf16[128,128]{1,0:T(8,128)(2,1)S(1)}, u32[]{:S(2)}, u32[]{:S(2)}) collective-permute-start(bf16[128,128]{1,0:T(8,128)(2,1)S(1)} %get-tuple-element.41), channel_id=1, source_target_pairs={{0,3},{1,2},{2,1},{3,0},{4,7},{5,6},{6,5},{7,4},{8,11},{9,10},{10,... | collective-permute-start | bytes 98312 | tf_op jit(solution)/shard_map/ppermute | solution.py:285
  9.7 22.1 %copy-start = (bf16[2,768,192]{1,2,0:T(8,128)(2,1)S(1)}, bf16[2,768,192]{1,2,0:T(8,128)(2,1)}, u32[]{:S(2)}) copy-start(bf16[2,768,192]{1,2,0:T(8,128)(2,1)} %param.31) | copy-start | bytes 1769476
  9.7 22.1 %copy-start.1 = (bf16[2,768,192]{1,2,0:T(8,128)(2,1)S(1)}, bf16[2,768,192]{1,2,0:T(8,128)(2,1)}, u32[]{:S(2)}) copy-start(bf16[2,768,192]{1,2,0:T(8,128)(2,1)} %param.32) | copy-start | bytes 1769476
  9.7 13.8 %all-to-all-start = ((bf16[32,8,2,128]{3,2,1,0:T(2,128)(2,1)}), bf16[32,8,2,128]{3,2,1,0:T(2,128)(2,1)S(1)}, u32[]{:S(2)}, u32[]{:S(2)}) async-start(bf16[32,8,2,128]{3,2,1,0:T(2,128)(2,1)} %bitcast.11), calls=%async_computation | async-start | bytes 262144 | tf_op jit(solution)/shard_map/all_to_all | solution.py:337
  14.9 3.8 %collective-permute-start.3 = (bf16[1,2,16,192]{3,2,1,0:T(8,128)(2,1)S(1)}, bf16[1,2,16,192]{3,2,1,0:T(8,128)(2,1)S(1)}, u32[]{:S(2)}, u32[]{:S(2)}) collective-permute-start(bf16[1,2,16,192]{3,2,1,0:T(8,128)(2,1)S(1)} %bitcast.23), channel_id=1, source_target_pairs={{0,4},{4,0},{8,12},{12,8},{16,20},{20,16},{24,28},{28,24},{1,5},{5... | collective-permute-start | bytes 36872 | tf_op jit(solution)/shard_map/ppermute | solution.py:353
  18.8 6.9 %collective-permute-start.4 = (bf16[2,2,16,192]{3,2,1,0:T(8,128)(2,1)S(1)}, bf16[2,2,16,192]{3,2,1,0:T(8,128)(2,1)S(1)}, u32[]{:S(2)}, u32[]{:S(2)}) collective-permute-start(bf16[2,2,16,192]{3,2,1,0:T(8,128)(2,1)S(1)} %pad_maximum_fusion), channel_id=1, source_target_pairs={{0,8},{4,12},{8,0},{12,4},{16,24},{20,28},{24,16},{28,20},{1,9},{5... | collective-permute-start | bytes 73736 | tf_op jit(solution)/shard_map/ppermute | solution.py:353
  20.9 4.8 %collective-permute-start.5 = (bf16[2,2,16,192]{3,2,1,0:T(8,128)(2,1)S(1)}, bf16[2,2,16,192]{3,2,1,0:T(8,128)(2,1)S(1)}, u32[]{:S(2)}, u32[]{:S(2)}) collective-permute-start(bf16[2,2,16,192]{3,2,1,0:T(8,128)(2,1)S(1)} %pad_maximum_fusion), channel_id=1, source_target_pairs={{0,16},{4,20},{8,24},{12,28},{16,0},{20,4},{24,8},{28,12},{1,17},{... | collective-permute-start | bytes 73736 | tf_op jit(solution)/shard_map/ppermute | solution.py:353
  23.4 5.7 %collective-permute-start.6 = (bf16[2,2,16,192]{3,2,1,0:T(8,128)(2,1)S(1)}, bf16[2,2,16,192]{3,2,1,0:T(8,128)(2,1)S(1)}, u32[]{:S(2)}, u32[]{:S(2)}) collective-permute-start(bf16[2,2,16,192]{3,2,1,0:T(8,128)(2,1)S(1)} %pad_maximum_fusion), channel_id=1, source_target_pairs={{0,24},{4,28},{8,16},{12,20},{16,8},{20,12},{24,0},{28,4},{1,25},{... | collective-permute-start | bytes 73736 | tf_op jit(solution)/shard_map/ppermute | solution.py:353
  29.2 11.0 %all-to-all-start.1 = ((bf16[32,9,2,128]{3,2,1,0:T(2,128)(2,1)}), bf16[32,9,2,128]{3,2,1,0:T(2,128)(2,1)S(1)}, u32[]{:S(2)}, u32[]{:S(2)}) async-start(bf16[32,9,2,128]{3,2,1,0:T(2,128)(2,1)} %bitcast.14), calls=%async_computation.1 | async-start | bytes 294912 | tf_op jit(solution)/shard_map/all_to_all | solution.py:365
  31.8 8.4 %copy-start.2 = (bf16[192,768]{1,0:T(8,128)(2,1)S(1)}, bf16[192,768]{1,0:T(8,128)(2,1)}, u32[]{:S(2)}) copy-start(bf16[192,768]{1,0:T(8,128)(2,1)} %out_w_ref.1) | copy-start | bytes 884740
  40.8 2.6 %collective-permute-start.7 = (bf16[16,192]{1,0:T(8,128)(2,1)S(1)}, bf16[16,192]{1,0:T(8,128)(2,1)S(1)}, u32[]{:S(2)}, u32[]{:S(2)}) collective-permute-start(bf16[16,192]{1,0:T(8,128)(2,1)S(1)} %get-tuple-element.57), channel_id=1, source_target_pairs={{0,1},{1,0},{2,3},{3,2},{4,5},{5,4},{6,7},{7,6},{8,9},{9,8},{10,11... | collective-permute-start | bytes 18440 | tf_op jit(solution)/shard_map/ppermute | solution.py:285
  41.1 3.7 %collective-permute-start.8 = (bf16[16,192]{1,0:T(8,128)(2,1)S(1)}, bf16[16,192]{1,0:T(8,128)(2,1)S(1)}, u32[]{:S(2)}, u32[]{:S(2)}) collective-permute-start(bf16[16,192]{1,0:T(8,128)(2,1)S(1)} %get-tuple-element.58), channel_id=1, source_target_pairs={{0,2},{1,3},{2,0},{3,1},{4,6},{5,7},{6,4},{7,5},{8,10},{9,11},{10,... | collective-permute-start | bytes 18440 | tf_op jit(solution)/shard_map/ppermute | solution.py:285
  41.4 3.3 %collective-permute-start.9 = (bf16[16,192]{1,0:T(8,128)(2,1)S(1)}, bf16[16,192]{1,0:T(8,128)(2,1)S(1)}, u32[]{:S(2)}, u32[]{:S(2)}) collective-permute-start(bf16[16,192]{1,0:T(8,128)(2,1)S(1)} %get-tuple-element.59), channel_id=1, source_target_pairs={{0,3},{1,2},{2,1},{3,0},{4,7},{5,6},{6,5},{7,4},{8,11},{9,10},{10,... | collective-permute-start | bytes 18440 | tf_op jit(solution)/shard_map/ppermute | solution.py:285
